TPU v7x, 32 devices: a whole 2x2x4 slice. The times are simulated.
32 devices in a mesh: gx: 4 (over z), gy: 8 (over y, x, core).
Axes of the slice: x: 2, y: 2, z: 4, core: 2. Of those that a mesh axis runs over, the one named last changes fastest.
Arguments:
- source: float32 [128, 256, 128], P('gx', 'gy'), may hold values from -6 to 6
- inverse_density: float32 [128, 256, 128], P('gx', 'gy'), may hold values from 1 to 7
Outputs:
- correction: float32 [128, 256, 128], P('gx', 'gy')
All inputs are finite; a program needn't handle non-finite values.
Results may differ from a plain program's by a relative error of at most 0.0001.
Values sent between devices are 32-bit elements; how exact they have to be, the bound alone decides.
A program may use at most 128 MiB of HBM per device.

v0:
```python
import jax
import jax.numpy as jnp
from jax import lax
from jax.sharding import PartitionSpec as P

LEVELS = 4
NU1 = 3
NU2 = 2
NC = 5


OMEGA = 0.8


def padded_2(value, sides, width):
    for axis, dim in sides:
        peers, length = (lax.axis_size(axis), value.shape[dim])
        up = [(i, (i + 1) % peers) for i in range(peers)]
        down = [(j, i) for i, j in up]
        last = lax.slice_in_dim(value, length - width, length, axis=dim)
        leading = lax.slice_in_dim(value, 0, width, axis=dim)
        before = lax.ppermute(last, axis, up)
        after = lax.ppermute(leading, axis, down)
        value = jnp.concatenate([before, value, after], axis=dim)
    return value


def from_behind(block, axis, distance):
    devices = range(lax.axis_size(axis))
    route = [((i - distance) % len(devices), i) for i in devices]
    return lax.ppermute(block, axis, route)


def partner_2(value, axis, apart):
    mask = 2**apart
    pairs = [(source, source ^ mask) for source in range(lax.axis_size(axis))]
    return lax.ppermute(value, axis, pairs)


def harmonic(left_value, right_value):
    return 2.0 * left_value * right_value / (left_value + right_value)


def centre_and_others(padded):
    centre = padded[1:-1, 1:-1, 1:-1]
    others = [
        padded[:-2, 1:-1, 1:-1],
        padded[2:, 1:-1, 1:-1],
        padded[1:-1, :-2, 1:-1],
        padded[1:-1, 2:, 1:-1],
        padded[1:-1, 1:-1, :-2],
        padded[1:-1, 1:-1, 2:],
    ]
    return (centre, others)


def coefficients(coef_padded, factor):
    centre, others = centre_and_others(coef_padded)
    couplings = [factor * harmonic(centre, neighbour) for neighbour in others]
    diagonal = (
        couplings[0] + couplings[1] + couplings[2] + couplings[3] + couplings[4] + couplings[5]
    )
    return (couplings, diagonal)


def residual_of(field_padded, source, couplings):
    centre, others = centre_and_others(field_padded)
    applied = couplings[0] * (centre - others[0])
    for position in range(1, 6):
        applied = applied + couplings[position] * (centre - others[position])
    return source - applied


def pad_depth(values, replicate_ends):
    if replicate_ends:
        return jnp.concatenate([values[:, :, :1], values, values[:, :, -1:]], axis=2)
    zero_layer = jnp.zeros(values.shape[:2] + (1,), jnp.float32)
    return jnp.concatenate([zero_layer, values, zero_layer], axis=2)


def rims_in_order(values, stride):
    widened = padded_2(values, (("gx", 0),), 1)
    from_below = from_behind(widened[:, -1:, :], "gy", stride)
    from_above = from_behind(widened[:, :1, :], "gy", -stride)
    return jnp.concatenate([from_below, widened, from_above], axis=1)


def with_rims(values, stride, replicate_ends):
    if stride == 1:
        widened = rims_in_order(values, stride)
    else:
        widened = rims_in_order(values, stride)
    return pad_depth(widened, replicate_ends)


def relax_once(iterate, source, couplings, diagonal, stride):
    padded = with_rims(iterate, stride, False)
    return iterate + OMEGA * residual_of(padded, source, couplings) / diagonal


def restrict(values):
    extent = values.shape
    return jnp.mean(
        values.reshape(extent[0] // 2, 2, extent[1] // 2, 2, extent[2] // 2, 2), axis=(1, 3, 5)
    )


def prolong(values):
    return jnp.repeat(jnp.repeat(jnp.repeat(values, 2, axis=0), 2, axis=1), 2, axis=2)


def merge_pairs(stacked, bit_number):
    partner = partner_2(stacked, "gy", bit_number)
    own_first = lax.axis_index("gy") // 2**bit_number % 2 == 0
    return jnp.where(
        own_first,
        jnp.concatenate([stacked, partner], axis=2),
        jnp.concatenate([partner, stacked], axis=2),
    )


def per_device(source, inverse_density):
    total_merges = lax.axis_size("gy").bit_length() - 2
    merge_counts = [0] * (LEVELS - 1) + [total_merges]
    records = []
    current_source, current_beta = (source, inverse_density)
    merged = 0
    for level_number in range(LEVELS):
        factor = 0.25**level_number
        coarsest = level_number == LEVELS - 1
        for bit_number in range(merged, merged + merge_counts[level_number]):
            stacked = merge_pairs(jnp.stack([current_source, current_beta]), bit_number)
            current_source, current_beta = (stacked[0], stacked[1])
        merged = merged + merge_counts[level_number]
        stride = 2**merged
        couplings, diagonal = coefficients(with_rims(current_beta, stride, True), factor)
        sweeps = NC if coarsest else NU1
        iterate = OMEGA * current_source / diagonal
        for sweep_number in range(sweeps - 1):
            iterate = relax_once(iterate, current_source, couplings, diagonal, stride)
        records.append((iterate, current_source, couplings, diagonal, stride, merged))
        if not coarsest:
            residual = residual_of(with_rims(iterate, stride, False), current_source, couplings)
            current_source = restrict(residual)
            current_beta = restrict(current_beta)
    correction = records[LEVELS - 1][0]
    gy_index = lax.axis_index("gy")
    for level_number in range(LEVELS - 2, -1, -1):
        iterate, level_source, couplings, diagonal, stride, done_here = records[level_number]
        done_next = records[level_number + 1][5]
        coarse_rows = iterate.shape[1] // 2
        tile_rows = coarse_rows // 2**done_here
        start_here = gy_index // 2**done_here * 2**done_here
        start_next = gy_index // 2**done_next * 2**done_next
        coarse_block = lax.dynamic_slice_in_dim(
            correction, (start_here - start_next) * tile_rows, coarse_rows, 1
        )
        iterate = iterate + prolong(coarse_block)
        for sweep_number in range(NU2):
            iterate = relax_once(iterate, level_source, couplings, diagonal, stride)
        correction = iterate
    return correction


def solution(mesh):
    placed = (P("gx", "gy", None), P("gx", "gy", None))
    return jax.shard_map(
        per_device, mesh=mesh, in_specs=placed, out_specs=P("gx", "gy", None), check_vma=False
    )
```

profile of v0, /device:TPU:0, one launch (start us, length us, event | category | flops | bytes accessed | tf_op | source)
XLA Modules:
  0.0 406.2 jit_solution(16819787105575292706)
XLA Ops:
  0.7 3.1 collective-permute-start
  3.8 2.0 collective-permute-start.1
  5.8 1.8 collective-permute-done
  8.8 2.6 collective-permute-start.3
  16.4 3.5 collective-permute-start.5
  19.8 34.9 %reshape.68 = f32[16,2,16,2,64,2]{5,4,3,2,1,0:T(8,128)} reshape(f32[32,32,128]{2,1,0:T(8,128)S(1)} %copy-done) | data formatting | bytes 1048576 | tf_op jit(solution)/shard_map/reshape | solution.py:104
  54.7 12.2 %reduce_sum.55 = f32[16,16,64]{2,1,0:T(8,128)S(1)} reduce(f32[16,2,16,2,64,2]{5,4,3,2,1,0:T(8,128)} %reshape.68, f32[]{:T(128)} %constant.92.clone.1), dimensions={1,3,5}, to_apply=%region_1.0 | reduce | flops 114688 | bytes 589828 | tf_op jit(solution)/shard_map/reduce_sum | solution.py:103
  68.3 2.4 collective-permute-start.7
  74.2 3.8 collective-permute-start.9
  78.0 3.8 collective-permute-start.17
  81.9 2.6 collective-permute-start.11
  84.7 2.6 collective-permute-start.19
  88.3 3.8 collective-permute-start.13
  93.9 2.6 collective-permute-start.15
  99.6 35.6 %reshape.67 = f32[16,2,16,2,64,2]{5,4,3,2,1,0:T(8,128)} reshape(f32[32,32,128]{2,1,0:T(8,128)} %fusion.24) | data formatting | bytes 1048576 | tf_op jit(solution)/shard_map/reshape | solution.py:104
  135.2 12.2 %reduce_sum.54 = f32[16,16,64]{2,1,0:T(8,128)S(1)} reduce(f32[16,2,16,2,64,2]{5,4,3,2,1,0:T(8,128)} %reshape.67, f32[]{:T(128)} %constant.92.clone.1), dimensions={1,3,5}, to_apply=%region_0.0 | reduce | flops 114688 | bytes 589828 | tf_op jit(solution)/shard_map/reduce_sum | solution.py:103
  147.4 2.7 fusion.219
  151.3 3.8 collective-permute-start.21
  155.2 6.5 %div.199 = f32[8,2,8,2,32,2]{5,4,3,2,1,0:T(8,128)} reshape(f32[16,16,64]{2,1,0:T(8,128)} %copy-done.13) | data formatting | bytes 131072 | tf_op jit(solution)/shard_map/div | solution.py:103
  161.7 3.2 reduce_sum.57
  165.9 2.6 collective-permute-start.23
  172.5 3.8 collective-permute-start.25
  176.3 3.8 collective-permute-start.33
  180.3 2.6 collective-permute-start.27
  183.0 2.6 collective-permute-start.35
  186.0 3.8 collective-permute-start.29
  191.6 2.6 collective-permute-start.31
  196.5 6.5 %reshape.69 = f32[8,2,8,2,32,2]{5,4,3,2,1,0:T(8,128)} reshape(f32[16,16,64]{2,1,0:T(8,128)} %fusion.133) | data formatting | bytes 131072 | tf_op jit(solution)/shard_map/reshape | solution.py:104
  203.0 3.2 reduce_sum.56
  207.6 3.9 collective-permute-start.37
  213.1 2.6 collective-permute-start.39
  219.2 2.8 collective-permute-start.41
  223.6 2.6 collective-permute-start.43
  229.9 2.7 collective-permute-start.45
  234.7 2.6 collective-permute-start.47
  237.3 1.9 div.216
  239.2 1.8 reduce_sum.59
  241.8 1.8 fusion.277
  243.5 1.9 reshape.70
  252.9 3.3 collective-permute-done.49
  258.4 2.7 collective-permute-start.51
  262.7 1.8 collective-permute-start.52
  269.8 2.7 collective-permute-start.55
  279.7 2.7 collective-permute-start.59
  283.9 1.8 collective-permute-start.60
  290.9 2.7 collective-permute-start.63
  301.4 3.0 collective-permute-start.67
  324.4 2.6 collective-permute-start.71
  328.7 2.6 collective-permute-start.73
  335.0 2.6 collective-permute-start.75
  339.2 2.6 collective-permute-start.77
  346.6 1.8 broadcast_in_dim.32
  348.4 1.9 copy.404
  352.7 2.7 collective-permute-start.79
  357.0 2.6 collective-permute-start.81
  363.8 2.7 collective-permute-start.83
  368.1 2.6 collective-permute-start.85
  373.5 2.8 copy.406
  376.3 2.9 broadcast_in_dim.35
  379.2 3.4 copy.407
  385.2 2.7 collective-permute-start.87
  389.7 2.6 collective-permute-start.89
  396.0 2.7 collective-permute-start.91
  400.4 2.6 collective-permute-start.93
  (364 shorter events, 137.8 us)
Async XLA Ops:
  0.7 6.9 %collective-permute-start = (f32[1,32,128]{2,1,0:T(8,128)S(1)}, f32[1,32,128]{2,1,0:T(8,128)S(1)}, u32[]{:S(2)}, u32[]{:S(2)}) collective-permute-start(f32[1,32,128]{2,1,0:T(8,128)S(1)} %get-tuple-element.53), channel_id=1, source_target_pairs={{0,8},{8,16},{16,24},{24,0},{1,9},{9,17},{17,25},{25,1},{2,10},{10... | collective-permute-start | bytes 49160 | tf_op jit(solution)/shard_map/ppermute | solution.py:22
  3.8 4.9 %collective-permute-start.1 = (f32[1,32,128]{2,1,0:T(8,128)S(1)}, f32[1,32,128]{2,1,0:T(8,128)S(1)}, u32[]{:S(2)}, u32[]{:S(2)}) collective-permute-start(f32[1,32,128]{2,1,0:T(8,128)S(1)} %get-tuple-element.52), channel_id=1, source_target_pairs={{8,0},{16,8},{24,16},{0,24},{9,1},{17,9},{25,17},{1,25},{10,2},{18... | collective-permute-start | bytes 49160 | tf_op jit(solution)/shard_map/ppermute | solution.py:23
  8.8 4.1 %collective-permute-start.2 = (f32[34,1,128]{2,1,0:T(1,128)S(1)}, f32[34,1,128]{2,1,0:T(1,128)S(1)}, u32[]{:S(2)}, u32[]{:S(2)}) collective-permute-start(f32[34,1,128]{2,1,0:T(1,128)S(1)} %get-tuple-element.41), channel_id=1, source_target_pairs={{7,0},{0,1},{1,2},{2,3},{3,4},{4,5},{5,6},{6,7},{15,8},{8,9},{9,10... | collective-permute-start | bytes 52232 | tf_op jit(solution)/shard_map/ppermute | solution.py:31
  8.8 4.1 %collective-permute-start.3 = (f32[34,1,128]{2,1,0:T(1,128)S(1)}, f32[34,1,128]{2,1,0:T(1,128)S(1)}, u32[]{:S(2)}, u32[]{:S(2)}) collective-permute-start(f32[34,1,128]{2,1,0:T(1,128)S(1)} %get-tuple-element.40), channel_id=1, source_target_pairs={{1,0},{2,1},{3,2},{4,3},{5,4},{6,5},{7,6},{0,7},{9,8},{10,9},{11,1... | collective-permute-start | bytes 52232 | tf_op jit(solution)/shard_map/ppermute | solution.py:31
  16.0 50.9 %collective-permute-start.4 = (f32[1,32,128]{2,1,0:T(8,128)S(1)}, f32[1,32,128]{2,1,0:T(8,128)S(1)}, u32[]{:S(2)}, u32[]{:S(2)}) collective-permute-start(f32[1,32,128]{2,1,0:T(8,128)S(1)} %get-tuple-element.50), channel_id=1, source_target_pairs={{0,8},{8,16},{16,24},{24,0},{1,9},{9,17},{17,25},{25,1},{2,10},{10... | collective-permute-start | bytes 49160 | tf_op jit(solution)/shard_map/ppermute | solution.py:22
  16.4 50.6 %collective-permute-start.5 = (f32[1,32,128]{2,1,0:T(8,128)S(1)}, f32[1,32,128]{2,1,0:T(8,128)S(1)}, u32[]{:S(2)}, u32[]{:S(2)}) collective-permute-start(f32[1,32,128]{2,1,0:T(8,128)S(1)} %get-tuple-element.51), channel_id=1, source_target_pairs={{8,0},{16,8},{24,16},{0,24},{9,1},{17,9},{25,17},{1,25},{10,2},{18... | collective-permute-start | bytes 49160 | tf_op jit(solution)/shard_map/ppermute | solution.py:23
  68.0 4.1 %collective-permute-start.6 = (f32[34,1,128]{2,1,0:T(1,128)S(1)}, f32[34,1,128]{2,1,0:T(1,128)S(1)}, u32[]{:S(2)}, u32[]{:S(2)}) collective-permute-start(f32[34,1,128]{2,1,0:T(1,128)S(1)} %get-tuple-element.38), channel_id=1, source_target_pairs={{7,0},{0,1},{1,2},{2,3},{3,4},{4,5},{5,6},{6,7},{15,8},{8,9},{9,10... | collective-permute-start | bytes 52232 | tf_op jit(solution)/shard_map/ppermute | solution.py:31
  74.1 7.7 %collective-permute-start.8 = (f32[1,32,128]{2,1,0:T(8,128)S(1)}, f32[1,32,128]{2,1,0:T(8,128)S(1)}, u32[]{:S(2)}, u32[]{:S(2)}) collective-permute-start(f32[1,32,128]{2,1,0:T(8,128)S(1)} %get-tuple-element.48), channel_id=1, source_target_pairs={{0,8},{8,16},{16,24},{24,0},{1,9},{9,17},{17,25},{25,1},{2,10},{10... | collective-permute-start | bytes 49160 | tf_op jit(solution)/shard_map/ppermute | solution.py:22
  74.2 7.6 %collective-permute-start.9 = (f32[1,32,128]{2,1,0:T(8,128)S(1)}, f32[1,32,128]{2,1,0:T(8,128)S(1)}, u32[]{:S(2)}, u32[]{:S(2)}) collective-permute-start(f32[1,32,128]{2,1,0:T(8,128)S(1)} %get-tuple-element.49), channel_id=1, source_target_pairs={{8,0},{16,8},{24,16},{0,24},{9,1},{17,9},{25,17},{1,25},{10,2},{18... | collective-permute-start | bytes 49160 | tf_op jit(solution)/shard_map/ppermute | solution.py:23
  78.0 6.6 %collective-permute-start.16 = (f32[1,16,64]{2,1,0:T(8,128)S(1)}, f32[1,16,64]{2,1,0:T(8,128)S(1)}, u32[]{:S(2)}, u32[]{:S(2)}) collective-permute-start(f32[1,16,64]{2,1,0:T(8,128)S(1)} %get-tuple-element.78), channel_id=1, source_target_pairs={{0,8},{8,16},{16,24},{24,0},{1,9},{9,17},{17,25},{25,1},{2,10},{10... | collective-permute-start | bytes 12296 | tf_op jit(solution)/shard_map/ppermute | solution.py:22
  78.0 6.6 %collective-permute-start.17 = (f32[1,16,64]{2,1,0:T(8,128)S(1)}, f32[1,16,64]{2,1,0:T(8,128)S(1)}, u32[]{:S(2)}, u32[]{:S(2)}) collective-permute-start(f32[1,16,64]{2,1,0:T(8,128)S(1)} %get-tuple-element.79), channel_id=1, source_target_pairs={{8,0},{16,8},{24,16},{0,24},{9,1},{17,9},{25,17},{1,25},{10,2},{18... | collective-permute-start | bytes 12296 | tf_op jit(solution)/shard_map/ppermute | solution.py:23
  81.9 5.4 %collective-permute-start.10 = (f32[34,1,128]{2,1,0:T(1,128)S(1)}, f32[34,1,128]{2,1,0:T(1,128)S(1)}, u32[]{:S(2)}, u32[]{:S(2)}) collective-permute-start(f32[34,1,128]{2,1,0:T(1,128)S(1)} %get-tuple-element.36), channel_id=1, source_target_pairs={{7,0},{0,1},{1,2},{2,3},{3,4},{4,5},{5,6},{6,7},{15,8},{8,9},{9,10... | collective-permute-start | bytes 52232 | tf_op jit(solution)/shard_map/ppermute | solution.py:31
  81.9 5.4 %collective-permute-start.11 = (f32[34,1,128]{2,1,0:T(1,128)S(1)}, f32[34,1,128]{2,1,0:T(1,128)S(1)}, u32[]{:S(2)}, u32[]{:S(2)}) collective-permute-start(f32[34,1,128]{2,1,0:T(1,128)S(1)} %get-tuple-element.37), channel_id=1, source_target_pairs={{1,0},{2,1},{3,2},{4,3},{5,4},{6,5},{7,6},{0,7},{9,8},{10,9},{11,1... | collective-permute-start | bytes 52232 | tf_op jit(solution)/shard_map/ppermute | solution.py:31
  84.6 7.5 %collective-permute-start.18 = (f32[18,1,64]{2,1,0:T(1,128)S(1)}, f32[18,1,64]{2,1,0:T(1,128)S(1)}, u32[]{:S(2)}, u32[]{:S(2)}) collective-permute-start(f32[18,1,64]{2,1,0:T(1,128)S(1)} %get-tuple-element.67), channel_id=1, source_target_pairs={{7,0},{0,1},{1,2},{2,3},{3,4},{4,5},{5,6},{6,7},{15,8},{8,9},{9,10... | collective-permute-start | bytes 13832 | tf_op jit(solution)/shard_map/ppermute | solution.py:31
  84.7 7.4 %collective-permute-start.19 = (f32[18,1,64]{2,1,0:T(1,128)S(1)}, f32[18,1,64]{2,1,0:T(1,128)S(1)}, u32[]{:S(2)}, u32[]{:S(2)}) collective-permute-start(f32[18,1,64]{2,1,0:T(1,128)S(1)} %get-tuple-element.66), channel_id=1, source_target_pairs={{1,0},{2,1},{3,2},{4,3},{5,4},{6,5},{7,6},{0,7},{9,8},{10,9},{11,1... | collective-permute-start | bytes 13832 | tf_op jit(solution)/shard_map/ppermute | solution.py:31
  88.2 5.6 %collective-permute-start.12 = (f32[1,32,128]{2,1,0:T(8,128)S(1)}, f32[1,32,128]{2,1,0:T(8,128)S(1)}, u32[]{:S(2)}, u32[]{:S(2)}) collective-permute-start(f32[1,32,128]{2,1,0:T(8,128)S(1)} %get-tuple-element.46), channel_id=1, source_target_pairs={{0,8},{8,16},{16,24},{24,0},{1,9},{9,17},{17,25},{25,1},{2,10},{10... | collective-permute-start | bytes 49160 | tf_op jit(solution)/shard_map/ppermute | solution.py:22
  88.3 5.5 %collective-permute-start.13 = (f32[1,32,128]{2,1,0:T(8,128)S(1)}, f32[1,32,128]{2,1,0:T(8,128)S(1)}, u32[]{:S(2)}, u32[]{:S(2)}) collective-permute-start(f32[1,32,128]{2,1,0:T(8,128)S(1)} %get-tuple-element.47), channel_id=1, source_target_pairs={{8,0},{16,8},{24,16},{0,24},{9,1},{17,9},{25,17},{1,25},{10,2},{18... | collective-permute-start | bytes 49160 | tf_op jit(solution)/shard_map/ppermute | solution.py:23
  93.9 4.1 %collective-permute-start.14 = (f32[34,1,128]{2,1,0:T(1,128)S(1)}, f32[34,1,128]{2,1,0:T(1,128)S(1)}, u32[]{:S(2)}, u32[]{:S(2)}) collective-permute-start(f32[34,1,128]{2,1,0:T(1,128)S(1)} %get-tuple-element.34), channel_id=1, source_target_pairs={{7,0},{0,1},{1,2},{2,3},{3,4},{4,5},{5,6},{6,7},{15,8},{8,9},{9,10... | collective-permute-start | bytes 52232 | tf_op jit(solution)/shard_map/ppermute | solution.py:31
  93.9 4.1 %collective-permute-start.15 = (f32[34,1,128]{2,1,0:T(1,128)S(1)}, f32[34,1,128]{2,1,0:T(1,128)S(1)}, u32[]{:S(2)}, u32[]{:S(2)}) collective-permute-start(f32[34,1,128]{2,1,0:T(1,128)S(1)} %get-tuple-element.35), channel_id=1, source_target_pairs={{1,0},{2,1},{3,2},{4,3},{5,4},{6,5},{7,6},{0,7},{9,8},{10,9},{11,1... | collective-permute-start | bytes 52232 | tf_op jit(solution)/shard_map/ppermute | solution.py:31
  151.3 13.5 %collective-permute-start.20 = (f32[1,16,64]{2,1,0:T(8,128)}, f32[1,16,64]{2,1,0:T(8,128)}, u32[]{:S(2)}, u32[]{:S(2)}) collective-permute-start(f32[1,16,64]{2,1,0:T(8,128)} %get-tuple-element.76), channel_id=1, source_target_pairs={{0,8},{8,16},{16,24},{24,0},{1,9},{9,17},{17,25},{25,1},{2,10},{10... | collective-permute-start | bytes 12296 | tf_op jit(solution)/shard_map/ppermute | solution.py:22
  151.3 13.5 %collective-permute-start.21 = (f32[1,16,64]{2,1,0:T(8,128)}, f32[1,16,64]{2,1,0:T(8,128)}, u32[]{:S(2)}, u32[]{:S(2)}) collective-permute-start(f32[1,16,64]{2,1,0:T(8,128)} %get-tuple-element.77), channel_id=1, source_target_pairs={{8,0},{16,8},{24,16},{0,24},{9,1},{17,9},{25,17},{1,25},{10,2},{18... | collective-permute-start | bytes 12296 | tf_op jit(solution)/shard_map/ppermute | solution.py:23
  172.5 7.7 %collective-permute-start.24 = (f32[1,16,64]{2,1,0:T(8,128)S(1)}, f32[1,16,64]{2,1,0:T(8,128)S(1)}, u32[]{:S(2)}, u32[]{:S(2)}) collective-permute-start(f32[1,16,64]{2,1,0:T(8,128)S(1)} %get-tuple-element.74), channel_id=1, source_target_pairs={{0,8},{8,16},{16,24},{24,0},{1,9},{9,17},{17,25},{25,1},{2,10},{10... | collective-permute-start | bytes 12296 | tf_op jit(solution)/shard_map/ppermute | solution.py:22
  172.5 7.6 %collective-permute-start.25 = (f32[1,16,64]{2,1,0:T(8,128)S(1)}, f32[1,16,64]{2,1,0:T(8,128)S(1)}, u32[]{:S(2)}, u32[]{:S(2)}) collective-permute-start(f32[1,16,64]{2,1,0:T(8,128)S(1)} %get-tuple-element.75), channel_id=1, source_target_pairs={{8,0},{16,8},{24,16},{0,24},{9,1},{17,9},{25,17},{1,25},{10,2},{18... | collective-permute-start | bytes 12296 | tf_op jit(solution)/shard_map/ppermute | solution.py:23
  176.3 6.6 %collective-permute-start.32 = (f32[1,8,32]{2,1,0:T(8,128)S(1)}, f32[1,8,32]{2,1,0:T(8,128)S(1)}, u32[]{:S(2)}, u32[]{:S(2)}) collective-permute-start(f32[1,8,32]{2,1,0:T(8,128)S(1)} %get-tuple-element.130), channel_id=1, source_target_pairs={{0,8},{8,16},{16,24},{24,0},{1,9},{9,17},{17,25},{25,1},{2,10},{10... | collective-permute-start | bytes 3080 | tf_op jit(solution)/shard_map/ppermute | solution.py:22
  176.3 6.6 %collective-permute-start.33 = (f32[1,8,32]{2,1,0:T(8,128)S(1)}, f32[1,8,32]{2,1,0:T(8,128)S(1)}, u32[]{:S(2)}, u32[]{:S(2)}) collective-permute-start(f32[1,8,32]{2,1,0:T(8,128)S(1)} %get-tuple-element.131), channel_id=1, source_target_pairs={{8,0},{16,8},{24,16},{0,24},{9,1},{17,9},{25,17},{1,25},{10,2},{18... | collective-permute-start | bytes 3080 | tf_op jit(solution)/shard_map/ppermute | solution.py:23
  180.2 5.4 %collective-permute-start.26 = (f32[18,1,64]{2,1,0:T(1,128)S(1)}, f32[18,1,64]{2,1,0:T(1,128)S(1)}, u32[]{:S(2)}, u32[]{:S(2)}) collective-permute-start(f32[18,1,64]{2,1,0:T(1,128)S(1)} %get-tuple-element.62), channel_id=1, source_target_pairs={{7,0},{0,1},{1,2},{2,3},{3,4},{4,5},{5,6},{6,7},{15,8},{8,9},{9,10... | collective-permute-start | bytes 13832 | tf_op jit(solution)/shard_map/ppermute | solution.py:31
  180.3 5.4 %collective-permute-start.27 = (f32[18,1,64]{2,1,0:T(1,128)S(1)}, f32[18,1,64]{2,1,0:T(1,128)S(1)}, u32[]{:S(2)}, u32[]{:S(2)}) collective-permute-start(f32[18,1,64]{2,1,0:T(1,128)S(1)} %get-tuple-element.63), channel_id=1, source_target_pairs={{1,0},{2,1},{3,2},{4,3},{5,4},{6,5},{7,6},{0,7},{9,8},{10,9},{11,1... | collective-permute-start | bytes 13832 | tf_op jit(solution)/shard_map/ppermute | solution.py:31
  182.9 6.9 %collective-permute-start.34 = (f32[10,1,32]{2,1,0:T(1,128)S(1)}, f32[10,1,32]{2,1,0:T(1,128)S(1)}, u32[]{:S(2)}, u32[]{:S(2)}) collective-permute-start(f32[10,1,32]{2,1,0:T(1,128)S(1)} %get-tuple-element.111), channel_id=1, source_target_pairs={{7,0},{0,1},{1,2},{2,3},{3,4},{4,5},{5,6},{6,7},{15,8},{8,9},{9,10... | collective-permute-start | bytes 3848 | tf_op jit(solution)/shard_map/ppermute | solution.py:31
  183.0 6.9 %collective-permute-start.35 = (f32[10,1,32]{2,1,0:T(1,128)S(1)}, f32[10,1,32]{2,1,0:T(1,128)S(1)}, u32[]{:S(2)}, u32[]{:S(2)}) collective-permute-start(f32[10,1,32]{2,1,0:T(1,128)S(1)} %get-tuple-element.110), channel_id=1, source_target_pairs={{1,0},{2,1},{3,2},{4,3},{5,4},{6,5},{7,6},{0,7},{9,8},{10,9},{11,1... | collective-permute-start | bytes 3848 | tf_op jit(solution)/shard_map/ppermute | solution.py:31
  186.0 5.5 %collective-permute-start.28 = (f32[1,16,64]{2,1,0:T(8,128)S(1)}, f32[1,16,64]{2,1,0:T(8,128)S(1)}, u32[]{:S(2)}, u32[]{:S(2)}) collective-permute-start(f32[1,16,64]{2,1,0:T(8,128)S(1)} %get-tuple-element.72), channel_id=1, source_target_pairs={{0,8},{8,16},{16,24},{24,0},{1,9},{9,17},{17,25},{25,1},{2,10},{10... | collective-permute-start | bytes 12296 | tf_op jit(solution)/shard_map/ppermute | solution.py:22
  186.0 5.4 %collective-permute-start.29 = (f32[1,16,64]{2,1,0:T(8,128)S(1)}, f32[1,16,64]{2,1,0:T(8,128)S(1)}, u32[]{:S(2)}, u32[]{:S(2)}) collective-permute-start(f32[1,16,64]{2,1,0:T(8,128)S(1)} %get-tuple-element.73), channel_id=1, source_target_pairs={{8,0},{16,8},{24,16},{0,24},{9,1},{17,9},{25,17},{1,25},{10,2},{18... | collective-permute-start | bytes 12296 | tf_op jit(solution)/shard_map/ppermute | solution.py:23
  207.6 5.5 %collective-permute-start.36 = (f32[1,8,32]{2,1,0:T(8,128)S(1)}, f32[1,8,32]{2,1,0:T(8,128)S(1)}, u32[]{:S(2)}, u32[]{:S(2)}) collective-permute-start(f32[1,8,32]{2,1,0:T(8,128)S(1)} %get-tuple-element.128), channel_id=1, source_target_pairs={{0,8},{8,16},{16,24},{24,0},{1,9},{9,17},{17,25},{25,1},{2,10},{10... | collective-permute-start | bytes 3080 | tf_op jit(solution)/shard_map/ppermute | solution.py:22
  207.6 5.4 %collective-permute-start.37 = (f32[1,8,32]{2,1,0:T(8,128)S(1)}, f32[1,8,32]{2,1,0:T(8,128)S(1)}, u32[]{:S(2)}, u32[]{:S(2)}) collective-permute-start(f32[1,8,32]{2,1,0:T(8,128)S(1)} %get-tuple-element.129), channel_id=1, source_target_pairs={{8,0},{16,8},{24,16},{0,24},{9,1},{17,9},{25,17},{1,25},{10,2},{18... | collective-permute-start | bytes 3080 | tf_op jit(solution)/shard_map/ppermute | solution.py:23
  218.0 5.5 %collective-permute-start.40 = (f32[1,8,32]{2,1,0:T(8,128)S(1)}, f32[1,8,32]{2,1,0:T(8,128)S(1)}, u32[]{:S(2)}, u32[]{:S(2)}) collective-permute-start(f32[1,8,32]{2,1,0:T(8,128)S(1)} %get-tuple-element.126), channel_id=1, source_target_pairs={{0,8},{8,16},{16,24},{24,0},{1,9},{9,17},{17,25},{25,1},{2,10},{10... | collective-permute-start | bytes 3080 | tf_op jit(solution)/shard_map/ppermute | solution.py:22
  219.2 4.3 %collective-permute-start.41 = (f32[1,8,32]{2,1,0:T(8,128)S(1)}, f32[1,8,32]{2,1,0:T(8,128)S(1)}, u32[]{:S(2)}, u32[]{:S(2)}) collective-permute-start(f32[1,8,32]{2,1,0:T(8,128)S(1)} %get-tuple-element.127), channel_id=1, source_target_pairs={{8,0},{16,8},{24,16},{0,24},{9,1},{17,9},{25,17},{1,25},{10,2},{18... | collective-permute-start | bytes 3080 | tf_op jit(solution)/shard_map/ppermute | solution.py:23
  228.5 5.5 %collective-permute-start.44 = (f32[1,8,32]{2,1,0:T(8,128)S(1)}, f32[1,8,32]{2,1,0:T(8,128)S(1)}, u32[]{:S(2)}, u32[]{:S(2)}) collective-permute-start(f32[1,8,32]{2,1,0:T(8,128)S(1)} %get-tuple-element.124), channel_id=1, source_target_pairs={{0,8},{8,16},{16,24},{24,0},{1,9},{9,17},{17,25},{25,1},{2,10},{10... | collective-permute-start | bytes 3080 | tf_op jit(solution)/shard_map/ppermute | solution.py:22
  229.9 4.2 %collective-permute-start.45 = (f32[1,8,32]{2,1,0:T(8,128)S(1)}, f32[1,8,32]{2,1,0:T(8,128)S(1)}, u32[]{:S(2)}, u32[]{:S(2)}) collective-permute-start(f32[1,8,32]{2,1,0:T(8,128)S(1)} %get-tuple-element.125), channel_id=1, source_target_pairs={{8,0},{16,8},{24,16},{0,24},{9,1},{17,9},{25,17},{1,25},{10,2},{18... | collective-permute-start | bytes 3080 | tf_op jit(solution)/shard_map/ppermute | solution.py:23
  234.7 6.3 %collective-permute-start.46 = (f32[10,1,32]{2,1,0:T(1,128)}, f32[10,1,32]{2,1,0:T(1,128)}, u32[]{:S(2)}, u32[]{:S(2)}) collective-permute-start(f32[10,1,32]{2,1,0:T(1,128)} %get-tuple-element.104), channel_id=1, source_target_pairs={{7,0},{0,1},{1,2},{2,3},{3,4},{4,5},{5,6},{6,7},{15,8},{8,9},{9,10... | collective-permute-start | bytes 3848 | tf_op jit(solution)/shard_map/ppermute | solution.py:31
  234.7 6.3 %collective-permute-start.47 = (f32[10,1,32]{2,1,0:T(1,128)}, f32[10,1,32]{2,1,0:T(1,128)}, u32[]{:S(2)}, u32[]{:S(2)}) collective-permute-start(f32[10,1,32]{2,1,0:T(1,128)} %get-tuple-element.105), channel_id=1, source_target_pairs={{1,0},{2,1},{3,2},{4,3},{5,4},{6,5},{7,6},{0,7},{9,8},{10,9},{11,1... | collective-permute-start | bytes 3848 | tf_op jit(solution)/shard_map/ppermute | solution.py:31
  252.0 4.2 %collective-permute-start.49 = (f32[2,4,8,16]{3,2,1,0:T(8,128)}, f32[2,4,8,16]{3,2,1,0:T(8,128)}, u32[]{:S(2)}, u32[]{:S(2)}) collective-permute-start(f32[2,4,8,16]{3,2,1,0:T(8,128)} %maximum_select_fusion.1), channel_id=1, source_target_pairs={{0,2},{1,3},{2,0},{3,1},{4,6},{5,7},{6,4},{7,5},{8,10},{9,11},{10,... | collective-permute-start | bytes 12296 | tf_op jit(solution)/shard_map/ppermute | solution.py:37
  257.1 5.6 %collective-permute-start.50 = (f32[1,16,16]{2,1,0:T(8,128)S(1)}, f32[1,16,16]{2,1,0:T(8,128)S(1)}, u32[]{:S(2)}, u32[]{:S(2)}) collective-permute-start(f32[1,16,16]{2,1,0:T(8,128)S(1)} %get-tuple-element.86), channel_id=1, source_target_pairs={{0,8},{8,16},{16,24},{24,0},{1,9},{9,17},{17,25},{25,1},{2,10},{10... | collective-permute-start | bytes 3080 | tf_op jit(solution)/shard_map/ppermute | solution.py:22
  258.4 4.2 %collective-permute-start.51 = (f32[1,16,16]{2,0,1:T(1,128)S(1)}, f32[1,16,16]{2,0,1:T(1,128)S(1)}, u32[]{:S(2)}, u32[]{:S(2)}) collective-permute-start(f32[1,16,16]{2,0,1:T(1,128)S(1)} %bitcast.55), channel_id=1, source_target_pairs={{8,0},{16,8},{24,16},{0,24},{9,1},{17,9},{25,17},{1,25},{10,2},{18... | collective-permute-start | bytes 3080 | tf_op jit(solution)/shard_map/ppermute | solution.py:23
  268.5 5.6 %collective-permute-start.54 = (f32[1,16,16]{2,0,1:T(1,128)S(1)}, f32[1,16,16]{2,0,1:T(1,128)S(1)}, u32[]{:S(2)}, u32[]{:S(2)}) collective-permute-start(f32[1,16,16]{2,0,1:T(1,128)S(1)} %get-tuple-element.122), channel_id=1, source_target_pairs={{0,8},{8,16},{16,24},{24,0},{1,9},{9,17},{17,25},{25,1},{2,10},{10... | collective-permute-start | bytes 3080 | tf_op jit(solution)/shard_map/ppermute | solution.py:22
  269.8 4.2 %collective-permute-start.55 = (f32[1,16,16]{2,0,1:T(1,128)S(1)}, f32[1,16,16]{2,0,1:T(1,128)S(1)}, u32[]{:S(2)}, u32[]{:S(2)}) collective-permute-start(f32[1,16,16]{2,0,1:T(1,128)S(1)} %get-tuple-element.123), channel_id=1, source_target_pairs={{8,0},{16,8},{24,16},{0,24},{9,1},{17,9},{25,17},{1,25},{10,2},{18... | collective-permute-start | bytes 3080 | tf_op jit(solution)/shard_map/ppermute | solution.py:23
  278.4 5.6 %collective-permute-start.58 = (f32[1,16,16]{2,0,1:T(1,128)S(1)}, f32[1,16,16]{2,0,1:T(1,128)S(1)}, u32[]{:S(2)}, u32[]{:S(2)}) collective-permute-start(f32[1,16,16]{2,0,1:T(1,128)S(1)} %get-tuple-element.120), channel_id=1, source_target_pairs={{0,8},{8,16},{16,24},{24,0},{1,9},{9,17},{17,25},{25,1},{2,10},{10... | collective-permute-start | bytes 3080 | tf_op jit(solution)/shard_map/ppermute | solution.py:22
  279.7 4.2 %collective-permute-start.59 = (f32[1,16,16]{2,0,1:T(1,128)S(1)}, f32[1,16,16]{2,0,1:T(1,128)S(1)}, u32[]{:S(2)}, u32[]{:S(2)}) collective-permute-start(f32[1,16,16]{2,0,1:T(1,128)S(1)} %get-tuple-element.121), channel_id=1, source_target_pairs={{8,0},{16,8},{24,16},{0,24},{9,1},{17,9},{25,17},{1,25},{10,2},{18... | collective-permute-start | bytes 3080 | tf_op jit(solution)/shard_map/ppermute | solution.py:23
  289.6 5.6 %collective-permute-start.62 = (f32[1,16,16]{2,0,1:T(1,128)S(1)}, f32[1,16,16]{2,0,1:T(1,128)S(1)}, u32[]{:S(2)}, u32[]{:S(2)}) collective-permute-start(f32[1,16,16]{2,0,1:T(1,128)S(1)} %get-tuple-element.118), channel_id=1, source_target_pairs={{0,8},{8,16},{16,24},{24,0},{1,9},{9,17},{17,25},{25,1},{2,10},{10... | collective-permute-start | bytes 3080 | tf_op jit(solution)/shard_map/ppermute | solution.py:22
  290.9 4.3 %collective-permute-start.63 = (f32[1,16,16]{2,0,1:T(1,128)S(1)}, f32[1,16,16]{2,0,1:T(1,128)S(1)}, u32[]{:S(2)}, u32[]{:S(2)}) collective-permute-start(f32[1,16,16]{2,0,1:T(1,128)S(1)} %get-tuple-element.119), channel_id=1, source_target_pairs={{8,0},{16,8},{24,16},{0,24},{9,1},{17,9},{25,17},{1,25},{10,2},{18... | collective-permute-start | bytes 3080 | tf_op jit(solution)/shard_map/ppermute | solution.py:23
  300.2 5.8 %collective-permute-start.66 = (f32[1,16,16]{2,0,1:T(1,128)}, f32[1,16,16]{2,0,1:T(1,128)}, u32[]{:S(2)}, u32[]{:S(2)}) collective-permute-start(f32[1,16,16]{2,0,1:T(1,128)} %get-tuple-element.116), channel_id=1, source_target_pairs={{0,8},{8,16},{16,24},{24,0},{1,9},{9,17},{17,25},{25,1},{2,10},{10... | collective-permute-start | bytes 3080 | tf_op jit(solution)/shard_map/ppermute | solution.py:22
  301.4 4.6 %collective-permute-start.67 = (f32[1,16,16]{2,0,1:T(1,128)}, f32[1,16,16]{2,0,1:T(1,128)}, u32[]{:S(2)}, u32[]{:S(2)}) collective-permute-start(f32[1,16,16]{2,0,1:T(1,128)} %get-tuple-element.117), channel_id=1, source_target_pairs={{8,0},{16,8},{24,16},{0,24},{9,1},{17,9},{25,17},{1,25},{10,2},{18... | collective-permute-start | bytes 3080 | tf_op jit(solution)/shard_map/ppermute | solution.py:23
  322.8 5.8 %collective-permute-start.70 = (f32[1,8,32]{2,1,0:T(8,128)S(1)}, f32[1,8,32]{2,1,0:T(8,128)S(1)}, u32[]{:S(2)}, u32[]{:S(2)}) collective-permute-start(f32[1,8,32]{2,1,0:T(8,128)S(1)} %get-tuple-element.114), channel_id=1, source_target_pairs={{0,8},{8,16},{16,24},{24,0},{1,9},{9,17},{17,25},{25,1},{2,10},{10... | collective-permute-start | bytes 3080 | tf_op jit(solution)/shard_map/ppermute | solution.py:22
  324.4 4.2 %collective-permute-start.71 = (f32[1,8,32]{2,1,0:T(8,128)S(1)}, f32[1,8,32]{2,1,0:T(8,128)S(1)}, u32[]{:S(2)}, u32[]{:S(2)}) collective-permute-start(f32[1,8,32]{2,1,0:T(8,128)S(1)} %get-tuple-element.115), channel_id=1, source_target_pairs={{8,0},{16,8},{24,16},{0,24},{9,1},{17,9},{25,17},{1,25},{10,2},{18... | collective-permute-start | bytes 3080 | tf_op jit(solution)/shard_map/ppermute | solution.py:23
  333.6 5.5 %collective-permute-start.74 = (f32[1,8,32]{2,1,0:T(8,128)S(1)}, f32[1,8,32]{2,1,0:T(8,128)S(1)}, u32[]{:S(2)}, u32[]{:S(2)}) collective-permute-start(f32[1,8,32]{2,1,0:T(8,128)S(1)} %get-tuple-element.112), channel_id=1, source_target_pairs={{0,8},{8,16},{16,24},{24,0},{1,9},{9,17},{17,25},{25,1},{2,10},{10... | collective-permute-start | bytes 3080 | tf_op jit(solution)/shard_map/ppermute | solution.py:22
  335.0 4.2 %collective-permute-start.75 = (f32[1,8,32]{2,1,0:T(8,128)S(1)}, f32[1,8,32]{2,1,0:T(8,128)S(1)}, u32[]{:S(2)}, u32[]{:S(2)}) collective-permute-start(f32[1,8,32]{2,1,0:T(8,128)S(1)} %get-tuple-element.113), channel_id=1, source_target_pairs={{8,0},{16,8},{24,16},{0,24},{9,1},{17,9},{25,17},{1,25},{10,2},{18... | collective-permute-start | bytes 3080 | tf_op jit(solution)/shard_map/ppermute | solution.py:23
  351.4 5.6 %collective-permute-start.78 = (f32[1,16,64]{2,1,0:T(8,128)S(1)}, f32[1,16,64]{2,1,0:T(8,128)S(1)}, u32[]{:S(2)}, u32[]{:S(2)}) collective-permute-start(f32[1,16,64]{2,1,0:T(8,128)S(1)} %get-tuple-element.70), channel_id=1, source_target_pairs={{0,8},{8,16},{16,24},{24,0},{1,9},{9,17},{17,25},{25,1},{2,10},{10... | collective-permute-start | bytes 12296 | tf_op jit(solution)/shard_map/ppermute | solution.py:22
  352.7 4.2 %collective-permute-start.79 = (f32[1,16,64]{2,1,0:T(8,128)S(1)}, f32[1,16,64]{2,1,0:T(8,128)S(1)}, u32[]{:S(2)}, u32[]{:S(2)}) collective-permute-start(f32[1,16,64]{2,1,0:T(8,128)S(1)} %get-tuple-element.71), channel_id=1, source_target_pairs={{8,0},{16,8},{24,16},{0,24},{9,1},{17,9},{25,17},{1,25},{10,2},{18... | collective-permute-start | bytes 12296 | tf_op jit(solution)/shard_map/ppermute | solution.py:23
  362.4 5.6 %collective-permute-start.82 = (f32[1,16,64]{2,1,0:T(8,128)S(1)}, f32[1,16,64]{2,1,0:T(8,128)S(1)}, u32[]{:S(2)}, u32[]{:S(2)}) collective-permute-start(f32[1,16,64]{2,1,0:T(8,128)S(1)} %get-tuple-element.68), channel_id=1, source_target_pairs={{0,8},{8,16},{16,24},{24,0},{1,9},{9,17},{17,25},{25,1},{2,10},{10... | collective-permute-start | bytes 12296 | tf_op jit(solution)/shard_map/ppermute | solution.py:22
  363.8 4.2 %collective-permute-start.83 = (f32[1,16,64]{2,1,0:T(8,128)S(1)}, f32[1,16,64]{2,1,0:T(8,128)S(1)}, u32[]{:S(2)}, u32[]{:S(2)}) collective-permute-start(f32[1,16,64]{2,1,0:T(8,128)S(1)} %get-tuple-element.69), channel_id=1, source_target_pairs={{8,0},{16,8},{24,16},{0,24},{9,1},{17,9},{25,17},{1,25},{10,2},{18... | collective-permute-start | bytes 12296 | tf_op jit(solution)/shard_map/ppermute | solution.py:23
  383.9 5.7 %collective-permute-start.86 = (f32[1,32,128]{2,1,0:T(8,128)S(1)}, f32[1,32,128]{2,1,0:T(8,128)S(1)}, u32[]{:S(2)}, u32[]{:S(2)}) collective-permute-start(f32[1,32,128]{2,1,0:T(8,128)S(1)} %get-tuple-element.44), channel_id=1, source_target_pairs={{0,8},{8,16},{16,24},{24,0},{1,9},{9,17},{17,25},{25,1},{2,10},{10... | collective-permute-start | bytes 49160 | tf_op jit(solution)/shard_map/ppermute | solution.py:22
  385.2 4.3 %collective-permute-start.87 = (f32[1,32,128]{2,1,0:T(8,128)S(1)}, f32[1,32,128]{2,1,0:T(8,128)S(1)}, u32[]{:S(2)}, u32[]{:S(2)}) collective-permute-start(f32[1,32,128]{2,1,0:T(8,128)S(1)} %get-tuple-element.45), channel_id=1, source_target_pairs={{8,0},{16,8},{24,16},{0,24},{9,1},{17,9},{25,17},{1,25},{10,2},{18... | collective-permute-start | bytes 49160 | tf_op jit(solution)/shard_map/ppermute | solution.py:23
  389.6 4.1 %collective-permute-start.88 = (f32[34,1,128]{2,1,0:T(1,128)S(1)}, f32[34,1,128]{2,1,0:T(1,128)S(1)}, u32[]{:S(2)}, u32[]{:S(2)}) collective-permute-start(f32[34,1,128]{2,1,0:T(1,128)S(1)} %get-tuple-element.32), channel_id=1, source_target_pairs={{7,0},{0,1},{1,2},{2,3},{3,4},{4,5},{5,6},{6,7},{15,8},{8,9},{9,10... | collective-permute-start | bytes 52232 | tf_op jit(solution)/shard_map/ppermute | solution.py:31
  394.7 5.7 %collective-permute-start.90 = (f32[1,32,128]{2,1,0:T(8,128)S(1)}, f32[1,32,128]{2,1,0:T(8,128)S(1)}, u32[]{:S(2)}, u32[]{:S(2)}) collective-permute-start(f32[1,32,128]{2,1,0:T(8,128)S(1)} %get-tuple-element.42), channel_id=1, source_target_pairs={{0,8},{8,16},{16,24},{24,0},{1,9},{9,17},{17,25},{25,1},{2,10},{10... | collective-permute-start | bytes 49160 | tf_op jit(solution)/shard_map/ppermute | solution.py:22
  396.0 4.3 %collective-permute-start.91 = (f32[1,32,128]{2,1,0:T(8,128)S(1)}, f32[1,32,128]{2,1,0:T(8,128)S(1)}, u32[]{:S(2)}, u32[]{:S(2)}) collective-permute-start(f32[1,32,128]{2,1,0:T(8,128)S(1)} %get-tuple-element.43), channel_id=1, source_target_pairs={{8,0},{16,8},{24,16},{0,24},{9,1},{17,9},{25,17},{1,25},{10,2},{18... | collective-permute-start | bytes 49160 | tf_op jit(solution)/shard_map/ppermute | solution.py:23
  400.4 4.1 %collective-permute-start.92 = (f32[34,1,128]{2,1,0:T(1,128)S(1)}, f32[34,1,128]{2,1,0:T(1,128)S(1)}, u32[]{:S(2)}, u32[]{:S(2)}) collective-permute-start(f32[34,1,128]{2,1,0:T(1,128)S(1)} %get-tuple-element.30), channel_id=1, source_target_pairs={{7,0},{0,1},{1,2},{2,3},{3,4},{4,5},{5,6},{6,7},{15,8},{8,9},{9,10... | collective-permute-start | bytes 52232 | tf_op jit(solution)/shard_map/ppermute | solution.py:31
  (79 other events, 981.5 us)
where the time goes:
time: 409 us; the launch traced here: 406 us
  starting transfers between devices  152 us (37%)
  local copies, waits for them, and re-layouts  118 us (29%)
  other arithmetic  74.5 us (18%)
  waiting for transfers between devices  60.8 us (15%)
    reshape x4, local copies, waits for them, and re-layouts, restrict(): values.reshape(extent[0] // 2, 2, extent[1] // 2, 2, extent[2] // 2, 2)  78.9 us
    ppermute x23, starting transfers between devices, padded_2(): after = lax.ppermute(leading, axis, down)  71.2 us
    ppermute x46, starting transfers between devices, from_behind(): return lax.ppermute(block, axis, route)  58.8 us
    reduce_sum x6, other arithmetic, restrict(): jnp.mean(values.reshape(extent[0] // 2, 2, extent[1] // 2, 2, extent[2] /...  34.2 us
    ppermute x46, waiting for transfers between devices, from_behind(): return lax.ppermute(block, axis, route)  29 us
    ppermute x23, waiting for transfers between devices, padded_2(): before = lax.ppermute(last, axis, up)  26.8 us
    ppermute x23, starting transfers between devices, padded_2(): before = lax.ppermute(last, axis, up)  21 us
    add x16, other arithmetic, relax_once(): return iterate + OMEGA * residual_of(padded, source, couplings) / diagonal  12.4 us
  transfers between devices with their start and end apart: 94, of which 42 were waited for; matrix products, arithmetic and copies ran while one was open for 16% of the time, Pallas kernels for 0%

commit v1 on v0

v1 whole, which is shorter than its diff:
```python
import functools

import jax
import jax.numpy as jnp
from jax import lax
from jax.experimental import pallas as pl
from jax.experimental.pallas import tpu as pltpu
from jax.sharding import PartitionSpec as P

MESH = pl.DeviceIdType.MESH
OMEGA = 0.8
F32 = jnp.float32

PLANES = (42, 28, 40, 20)
ROWS = (48, 32, 40, 24)
X_AT = (5, 6, 16, 8)
Y_AT = (8, 8, 16, 8)
OWN = 32
NEAR = [(dx, dy) for dx in (1, -1, 0) for dy in (0, 1, -1) if (dx, dy) != (0, 0)]


def far_offsets(peers):
    return (-1, 0, 1, 2) if peers == 4 else (-2, -1, 0, 1, 2)


def far_slot(peers, offset):
    return (offset + 2) % 4 if peers == 4 else offset + 2


def lanes(value, shift):
    return pltpu.roll(value, shift % 128, 1)


def rows(value, shift):
    return pltpu.roll(value, shift % value.shape[0], 0)


def lane_index(height):
    return lax.broadcasted_iota(jnp.int32, (height, 128), 1)


def swap_lanes(value, step):
    low = (lane_index(value.shape[0]) & step) == 0
    return jnp.where(low, lanes(value, -step), lanes(value, step))


def loop(first, last, body, unroll=2):
    count = last - first
    whole = count // unroll

    def step(trip, carry):
        for inner in range(unroll):
            body(first + trip * unroll + inner)
        return carry

    lax.fori_loop(0, whole, step, 0)
    for index in range(first + whole * unroll, last):
        body(index)


def build(level, b, f, cx, cy, cz, diag, gain, u):
    height = ROWS[level]
    factor2 = 2.0 * 0.25**level
    step = 2**level
    lane = lane_index(height)
    top = lane >= 128 - step
    ends = top | (lane < step)

    def pair(left, right):
        return factor2 * left * right / (left + right)

    def one(x, carry):
        before, here = carry
        after = b[x + 1]
        c_x = pair(here, after)
        c_y = pair(here, rows(here, -1))
        c_z = jnp.where(top, 0.0, pair(here, lanes(here, -step)))
        total = before + c_x + c_y + rows(c_y, 1) + c_z + lanes(c_z, step)
        total = total + jnp.where(ends, (0.5 * factor2) * here, 0.0)
        scaled = OMEGA / total
        cx[x] = c_x
        cy[x] = c_y
        cz[x] = c_z
        diag[x] = total
        gain[x] = scaled
        u[x] = scaled * f[x]
        return (c_x, after)

    first = pair(b[0], b[1])
    cx[0] = first

    def two(trip, carry):
        carry = one(1 + 2 * trip, carry)
        return one(2 + 2 * trip, carry)

    lax.fori_loop(0, (PLANES[level] - 2) // 2, two, (first, b[1]))


def spread(level, x, u, cx, cy, cz, span):
    here = u[x, span]
    along_y = cy[x, span]
    along_z = cz[x, span]
    step = 2**level
    total = cx[x, span] * u[x + 1, span] + cx[x - 1, span] * u[x - 1, span]
    total = total + (along_y * rows(here, -1) + rows(along_y * here, 1))
    total = total + (along_z * lanes(here, -step) + lanes(along_z * here, step))
    return here, total


def sweep(level, first, last, source, target, f, cx, cy, cz, gain, span=None):
    span = pl.ds(0, ROWS[level]) if span is None else span

    def one(x):
        here, total = spread(level, x, source, cx, cy, cz, span)
        target[x, span] = (1.0 - OMEGA) * here + gain[x, span] * (f[x, span] + total)

    loop(first, last, one)


def pair_mean(level, tmp, slot, value, count):
    tmp[slot, pl.ds(0, 2 * count)] = value
    summed = tmp[slot, pl.ds(0, count, stride=2)] + tmp[slot, pl.ds(1, count, stride=2)]
    return 0.125 * (summed + swap_lanes(summed, 2**level))


def restrict_field(level, b, target, tmp, fine_x, planes, fine_row, count, at_x, at_row):
    span = pl.ds(fine_row, 2 * count)

    def one(i):
        value = b[fine_x + 2 * i, span] + b[fine_x + 2 * i + 1, span]
        target[at_x + i, pl.ds(at_row, count)] = pair_mean(level, tmp, i, value, count)

    loop(0, planes, one)


def restrict_residual(level, u, f, cx, cy, cz, diag, target, tmp, fine_x, planes, fine_row, count, at_x, at_row):
    span = pl.ds(0, ROWS[level])

    def left(x):
        here, total = spread(level, x, u, cx, cy, cz, span)
        return f[x] + total - diag[x] * here

    def one(i):
        value = (left(fine_x + 2 * i) + left(fine_x + 2 * i + 1))[fine_row : fine_row + 2 * count]
        target[at_x + i, pl.ds(at_row, count)] = pair_mean(level, tmp, i, value, count)

    loop(0, planes, one, 1)


def add_coarse(u, coarse, tmp, first, planes, coarse_x, coarse_row, fine_row, count):
    def one(i):
        value = coarse[coarse_x + i, pl.ds(coarse_row, count)]
        tmp[i, pl.ds(0, count, stride=2)] = value
        tmp[i, pl.ds(1, count, stride=2)] = value
        both = tmp[i, pl.ds(0, 2 * count)]
        span = pl.ds(fine_row, 2 * count)
        u[first + 2 * i, span] = u[first + 2 * i, span] + both
        u[first + 2 * i + 1, span] = u[first + 2 * i + 1, span] + both

    loop(0, planes, one)


def pack_1(wide, packed):
    even = (lane_index(16) & 1) == 0
    span = pl.ds(8, 16)

    def one(i):
        packed[3 + i, span] = jnp.where(even, wide[6 + 2 * i, span], wide[7 + 2 * i, span])

    loop(0, 8, one)


def unpack_1(packed, wide):
    even = (lane_index(32) & 1) == 0

    def one(i):
        value = packed[i]
        other = swap_lanes(value, 1)
        wide[2 * i] = jnp.where(even, value, other)
        wide[2 * i + 1] = jnp.where(even, other, value)

    loop(0, 14, one)


def pack_2(wide, packed, slot):
    lane = lane_index(8)
    span = pl.ds(16, 8)
    for p in range(2):
        at = 16 + 4 * p
        low = jnp.where((lane & 1) == 0, wide[at, span], wide[at + 1, span])
        high = jnp.where((lane & 1) == 0, wide[at + 2, span], wide[at + 3, span])
        packed[slot, p] = jnp.where((lane & 2) == 0, low, high)


def unpack_2(nx, ny, packed, wide):
    lane = lane_index(8)
    even = (lane & 1) == 0
    low = (lane & 2) == 0

    def one(trip, carry):
        block = trip // 2
        part = trip % 2
        slot_x = block % 4 if nx == 4 else block
        for j in range(5):
            slot = slot_x * 5 + far_slot(ny, j - 2)
            value = packed[slot, part]
            other = swap_lanes(value, 2)
            span = pl.ds(8 * j, 8)
            for half, kept in enumerate((jnp.where(low, value, other), jnp.where(low, other, value))):
                swapped = swap_lanes(kept, 1)
                wide[4 * trip + 2 * half, span] = jnp.where(even, kept, swapped)
                wide[4 * trip + 2 * half + 1, span] = jnp.where(even, swapped, kept)
        return carry

    lax.fori_loop(0, 10, one, 0)


def side(offset, length, width, at):
    if offset == 0:
        return pl.ds(0, length), pl.ds(at, length)
    if offset == 1:
        return pl.ds(length - width, width), pl.ds(at - width, width)
    return pl.ds(0, width), pl.ds(at + length, width)


def kernel(nx, ny, f_in, b_in, out, *refs):
    fields = [refs[9 * level : 9 * level + 9] for level in range(4)]
    tmp, pf1, pb1, pf2, pb2, load_sem, send_sem, recv_sem = refs[36:]
    (b0, f0, u0, v0, cx0, cy0, cz0, d0, g0) = fields[0]
    (b1, f1, u1, v1, cx1, cy1, cz1, d1, g1) = fields[1]
    (b2, f2, u2, v2, cx2, cy2, cz2, d2, g2) = fields[2]
    (b3, f3, u3, v3, cx3, cy3, cz3, d3, g3) = fields[3]
    mx, my = lax.axis_index("gx"), lax.axis_index("gy")
    far = [(dx, dy) for dx in far_offsets(nx) for dy in far_offsets(ny) if (dx, dy) != (0, 0)]

    def peer(dx, dy):
        return (lax.rem(mx + dx + nx, nx), lax.rem(my + dy + ny, ny))

    barrier = pltpu.get_barrier_semaphore()
    greet = sorted(set(far) | set((-dx, -dy) for dx, dy in far))
    for dx, dy in greet:
        pl.semaphore_signal(barrier, inc=1, device_id=peer(dx, dy), device_id_type=MESH)

    inside = (pl.ds(5, OWN), pl.ds(8, OWN))
    load_b = pltpu.make_async_copy(b_in, b0.at[inside], load_sem.at[0])
    load_f = pltpu.make_async_copy(f_in, f0.at[inside], load_sem.at[1])
    load_b.start()
    load_f.start()
    pl.semaphore_wait(barrier, len(greet))

    started = []

    def send(source, target, dx, dy):
        number = len(started)
        copy = pltpu.make_async_remote_copy(
            src_ref=source,
            dst_ref=target,
            send_sem=send_sem.at[number],
            recv_sem=recv_sem.at[number],
            device_id=peer(dx, dy),
            device_id_type=MESH,
        )
        copy.start()
        started.append(copy)
        return copy

    fine = []
    for dx, dy in NEAR:
        for source, target, width in ((b_in, b0, 5), (f_in, f0, 4)):
            from_x, to_x = side(dx, OWN, width - (dy != 0), 5)
            from_y, to_y = side(dy, OWN, 8, 8)
            fine.append(send(source.at[from_x, from_y], target.at[to_x, to_y], dx, dy))

    def send_1(packed):
        copies = []
        for dx, dy in NEAR:
            from_x, to_x = side(dx, 8, 3, 3)
            from_y, to_y = side(dy, 16, 8, 8)
            from_x = pl.ds(from_x.start + 3, from_x.size)
            from_y = pl.ds(from_y.start + 8, from_y.size)
            copies.append(send(packed.at[from_x, from_y], packed.at[to_x, to_y], dx, dy))
        return copies

    def slot_2(dx, dy):
        return far_slot(nx, dx) * 5 + far_slot(ny, dy)

    def send_2(packed):
        return [send(packed.at[slot_2(0, 0)], packed.at[slot_2(-dx, -dy)], dx, dy) for dx, dy in far]

    load_b.wait()
    restrict_field(0, b0, b1, tmp, 5, 16, 8, 16, 6, 8)
    pack_1(b1, pb1)
    middle_b = send_1(pb1)
    restrict_field(1, b1, b2, tmp, 6, 8, 8, 8, 16, 16)
    pack_2(b2, pb2, slot_2(0, 0))
    coarse_b = send_2(pb2)
    load_f.wait()
    for copy in fine:
        copy.wait_recv()

    build(0, b0, f0, cx0, cy0, cz0, d0, g0, u0)
    sweep(0, 2, 40, u0, v0, f0, cx0, cy0, cz0, g0)
    sweep(0, 3, 39, v0, u0, f0, cx0, cy0, cz0, g0)
    restrict_residual(0, u0, f0, cx0, cy0, cz0, d0, f1, tmp, 5, 16, 8, 16, 6, 8)
    pack_1(f1, pf1)
    middle_f = send_1(pf1)
    for copy in middle_b:
        copy.wait_recv()
    unpack_1(pb1, b1)
    for copy in middle_f:
        copy.wait_recv()
    unpack_1(pf1, f1)

    build(1, b1, f1, cx1, cy1, cz1, d1, g1, u1)
    sweep(1, 2, 26, u1, v1, f1, cx1, cy1, cz1, g1)
    sweep(1, 3, 25, v1, u1, f1, cx1, cy1, cz1, g1)
    restrict_residual(1, u1, f1, cx1, cy1, cz1, d1, f2, tmp, 6, 8, 8, 8, 16, 16)
    pack_2(f2, pf2, slot_2(0, 0))
    coarse_f = send_2(pf2)
    for copy in coarse_b:
        copy.wait_recv()
    unpack_2(nx, ny, pb2, b2)
    restrict_field(2, b2, b3, tmp, 0, 20, 0, 20, 0, 0)
    for copy in coarse_f:
        copy.wait_recv()
    unpack_2(nx, ny, pf2, f2)

    build(2, b2, f2, cx2, cy2, cz2, d2, g2, u2)
    sweep(2, 2, 38, u2, v2, f2, cx2, cy2, cz2, g2)
    sweep(2, 3, 37, v2, u2, f2, cx2, cy2, cz2, g2)
    restrict_residual(2, u2, f2, cx2, cy2, cz2, d2, f3, tmp, 4, 16, 0, 20, 2, 0)

    build(3, b3, f3, cx3, cy3, cz3, d3, g3, u3)
    sweep(3, 3, 17, u3, v3, f3, cx3, cy3, cz3, g3)
    sweep(3, 4, 16, v3, u3, f3, cx3, cy3, cz3, g3)
    sweep(3, 5, 15, u3, v3, f3, cx3, cy3, cz3, g3)
    sweep(3, 6, 14, v3, u3, f3, cx3, cy3, cz3, g3)

    add_coarse(u2, u3, tmp, 12, 8, 6, 4, 8, 12)
    middle = pl.ds(8, 24)
    sweep(2, 13, 27, u2, v2, f2, cx2, cy2, cz2, g2, middle)
    sweep(2, 14, 26, v2, u2, f2, cx2, cy2, cz2, g2, middle)

    add_coarse(u1, u2, tmp, 2, 12, 14, 12, 0, 16)
    sweep(1, 4, 24, u1, v1, f1, cx1, cy1, cz1, g1)
    sweep(1, 5, 23, v1, u1, f1, cx1, cy1, cz1, g1)

    add_coarse(u0, u1, tmp, 3, 18, 5, 4, 0, 24)
    sweep(0, 4, 38, u0, v0, f0, cx0, cy0, cz0, g0)

    whole = pl.ds(0, ROWS[0])

    def last(x):
        here, total = spread(0, x, v0, cx0, cy0, cz0, whole)
        value = (1.0 - OMEGA) * here + g0[x] * (f0[x] + total)
        out[x - 5] = value[8:40]

    loop(5, 37, last)
    for copy in started:
        copy.wait_send()


def solution(mesh):
    nx, ny = mesh.shape["gx"], mesh.shape["gy"]
    far = len(far_offsets(nx)) * len(far_offsets(ny)) - 1
    copies = 4 * len(NEAR) + 2 * far
    shapes = []
    for planes, height in zip(PLANES, ROWS):
        shapes += [pltpu.VMEM((planes, height, 128), F32)] * 9

    def per_device(source, inverse_density):
        return pl.pallas_call(
            functools.partial(kernel, nx, ny),
            out_shape=jax.ShapeDtypeStruct(source.shape, F32),
            in_specs=[pl.BlockSpec(memory_space=pl.ANY)] * 2,
            out_specs=pl.BlockSpec(memory_space=pltpu.VMEM),
            scratch_shapes=shapes
            + [
                pltpu.VMEM((20, 48, 128), F32),
                pltpu.VMEM((14, 32, 128), F32),
                pltpu.VMEM((14, 32, 128), F32),
                pltpu.VMEM((25, 2, 8, 128), F32),
                pltpu.VMEM((25, 2, 8, 128), F32),
                pltpu.SemaphoreType.DMA((2,)),
                pltpu.SemaphoreType.DMA((copies,)),
                pltpu.SemaphoreType.DMA((copies,)),
            ],
            compiler_params=pltpu.CompilerParams(collective_id=0, has_side_effects=True),
        )(source, inverse_density)

    placed = (P("gx", "gy", None), P("gx", "gy", None))
    return jax.shard_map(
        per_device, mesh=mesh, in_specs=placed, out_specs=P("gx", "gy", None), check_vma=False
    )
```

time: 409 us -> 70.5 us (0.17)
  starting transfers between devices: 152 us -> 0 us
  local copies, waits for them, and re-layouts: 118 us -> 1.87 us
  other arithmetic: 74.5 us -> 0 us
  Pallas kernels: 0 us -> 68.5 us
  waiting for transfers between devices: 60.8 us -> 0 us
    ppermute x94 -> x0, starting transfers between devices: 152 us -> none  [the longest x23 71.2 us: padded_2(): after = lax.ppermute(leading, axis, down)]
    reshape x10 -> x0, local copies, waits for them, and re-layouts: 91.9 us -> none  [the longest x4 78.9 us: restrict(): values.reshape(extent[0] // 2, 2, extent[1] // 2, 2, extent[2] // 2, 2)]
    pallas_call x0 -> x1, Pallas kernels: none -> 68.5 us  [per_device(): pl.pallas_call(functools.partial(kernel, nx, ny), out_shape=jax.ShapeDtyp...]
    ppermute x94 -> x0, waiting for transfers between devices: 60.8 us -> none  [the longest x46 29 us: from_behind(): return lax.ppermute(block, axis, route)]
    reduce_sum x6 -> x0, other arithmetic: 34.2 us -> none  [restrict(): jnp.mean(values.reshape(extent[0] // 2, 2, extent[1] // 2, 2, extent[2] /...]
    add x20 -> x0, other arithmetic: 16.9 us -> none  [the longest x16 12.4 us: relax_once(): return iterate + OMEGA * residual_of(padded, source, couplings) / diagonal]
    broadcast_in_dim x9 -> x0, local copies, waits for them, and re-layouts: 8.44 us -> none  [the longest x3 6.15 us: prolong(): jnp.repeat(jnp.repeat(jnp.repeat(values, 2, axis=0), 2, axis=1), 2, axis=2)]
    div x2 -> x0, local copies, waits for them, and re-layouts: 8.38 us -> none  [restrict(): jnp.mean(values.reshape(extent[0] // 2, 2, extent[1] // 2, 2, extent[2] /...]
  transfers between devices with their start and end apart: 94 -> 0, of which waited for: 42 -> 0; matrix products, arithmetic and copies ran while one was open for 16% -> 0% of each run, Pallas kernels for 0% -> 0%
where the time goes in v1:
time: 70.5 us; the launch traced here: 70.3 us
  Pallas kernels  68.5 us (97%)
  local copies, waits for them, and re-layouts  1.87 us (3%)
    pallas_call x1, Pallas kernels, per_device(): pl.pallas_call(functools.partial(kernel, nx, ny), out_shape=jax.ShapeDtyp...  68.5 us
    unnamed x1, local copies, waits for them, and re-layouts  1.87 us

profile of v1, /device:TPU:0, one launch (start us, length us, event | category | flops | bytes accessed | tf_op | source)
XLA Modules:
  0.0 70.3 jit_solution(4570265947859682299)
XLA Ops:
  0.0 68.5 %shard_map.28 = f32[32,32,128]{2,1,0:T(8,128)} custom-call(f32[32,32,128]{2,1,0:T(8,128)} %f_in.1, f32[32,32,128]{2,1,0:T(8,128)} %b_in.1), custom_call_target="tpu_custom_call" | custom-call | tf_op jit(solution)/shard_map/pallas_call | solution.py:372
  68.5 1.9 %copy.4 = f32[32,32,128]{2,1,0:T(8,128)} copy(f32[32,32,128]{2,1,0:T(8,128)} %shard_map.28) | data formatting | bytes 1048576

commit v2 on v1

v2 whole, which is shorter than its diff:
```python
import functools

import jax
import jax.numpy as jnp
from jax import lax
from jax.experimental import pallas as pl
from jax.experimental.pallas import tpu as pltpu
from jax.sharding import PartitionSpec as P

MESH = pl.DeviceIdType.MESH
OMEGA = 0.8
F32 = jnp.float32

PLANES = (42, 16, 12, 5)
ROWS = (48, 32, 40, 24)
OWN = 32
NEAR = [(dx, dy) for dx in (1, -1, 0) for dy in (0, 1, -1) if (dx, dy) != (0, 0)]


def far_offsets(peers):
    return (-1, 0, 1, 2) if peers == 4 else (-2, -1, 0, 1, 2)


def lanes(value, shift):
    return pltpu.roll(value, shift % 128, 1)


def rows(value, shift):
    return pltpu.roll(value, shift % value.shape[0], 0)


def lane_index(height):
    return lax.broadcasted_iota(jnp.int32, (height, 128), 1)


def swap_lanes(value, step):
    low = (lane_index(value.shape[0]) & step) == 0
    return jnp.where(low, lanes(value, -step), lanes(value, step))


def loop(first, last, body, unroll=2):
    count = last - first
    whole = count // unroll

    def step(trip, carry):
        for inner in range(unroll):
            body(first + trip * unroll + inner)
        return carry

    lax.fori_loop(0, whole, step, 0)
    for index in range(first + whole * unroll, last):
        body(index)


def bit(number, height):
    return (lane_index(height) & number) != 0


def place_in_group(level, height):
    return lane_index(height) & (2**level - 1)


def next_x(level, here, after):
    if level == 0:
        return after
    size = 2**level
    last = place_in_group(level, here.shape[0]) == size - 1
    return jnp.where(last, lanes(after, size - 1), lanes(here, -1))


def previous_x(level, here, before):
    if level == 0:
        return before
    size = 2**level
    first = place_in_group(level, here.shape[0]) == 0
    return jnp.where(first, lanes(before, 1 - size), lanes(here, 1))


def build(level, b, f, cx, cxm, cy, cz, diag, gain, u):
    height = ROWS[level]
    factor2 = 2.0 * 0.25**level
    step = 2**level
    lane = lane_index(height)
    top = lane >= 128 - step
    ends = top | (lane < step)

    def pair(left, right):
        return factor2 * left * right / (left + right)

    def one(x, carry):
        c_before, here = carry
        after = b[x + 1]
        c_x = pair(here, next_x(level, here, after))
        c_m = previous_x(level, c_x, c_before)
        c_y = pair(here, rows(here, -1))
        c_z = jnp.where(top, 0.0, pair(here, lanes(here, -step)))
        total = c_m + c_x + c_y + rows(c_y, 1) + c_z + lanes(c_z, step)
        total = total + jnp.where(ends, (0.5 * factor2) * here, 0.0)
        scaled = OMEGA / total
        cx[x] = c_x
        if level > 0:
            cxm[x] = c_m
        cy[x] = c_y
        cz[x] = c_z
        diag[x] = total
        gain[x] = scaled
        u[x] = scaled * f[x]
        return (c_x, after)

    first = pair(b[0], next_x(level, b[0], b[1]))
    cx[0] = first
    count = PLANES[level] - 2
    carry = (first, b[1])
    if level == 3:
        for x in range(1, 1 + count):
            carry = one(x, carry)
        return

    def two(trip, carry):
        carry = one(1 + 2 * trip, carry)
        return one(2 + 2 * trip, carry)

    lax.fori_loop(0, count // 2, two, carry)


def spread(level, x, u, cx, cxm, cy, cz, span):
    here = u[x, span]
    along_y = cy[x, span]
    along_z = cz[x, span]
    step = 2**level
    lower = cx[x - 1, span] if level == 0 else cxm[x, span]
    total = cx[x, span] * next_x(level, here, u[x + 1, span])
    total = total + lower * previous_x(level, here, u[x - 1, span])
    total = total + (along_y * rows(here, -1) + rows(along_y * here, 1))
    total = total + (along_z * lanes(here, -step) + lanes(along_z * here, step))
    return here, total


def sweep(level, first, last, source, target, f, cx, cxm, cy, cz, gain, span=None):
    span = pl.ds(0, ROWS[level]) if span is None else span

    def one(x):
        here, total = spread(level, x, source, cx, cxm, cy, cz, span)
        target[x, span] = (1.0 - OMEGA) * here + gain[x, span] * (f[x, span] + total)

    if level == 3:
        for x in range(first, last):
            one(x)
    else:
        loop(first, last, one)


def coarsen(level, values):
    height = values[0].shape[0]
    if level == 0:
        even = ~bit(1, height)
        left, right = values[0] + values[1], values[2] + values[3]
        return jnp.where(even, left, right) + jnp.where(even, lanes(left, -1), lanes(right, 1))
    size = 2**level
    sums = []
    for value in values:
        value = value + swap_lanes(value, 1)
        value = value + swap_lanes(value, size)
        if level == 2:
            value = jnp.where(bit(2, height) == bit(1, height), value, swap_lanes(value, 2))
        sums.append(value)
    low, high = (1, 2) if level == 1 else (2, 4)
    lower = jnp.where(bit(low, height), sums[1], sums[0])
    upper = jnp.where(bit(low, height), sums[3], sums[2])
    return jnp.where(bit(high, height), upper, lower)


def refine(level, value):
    height = value.shape[0]
    if level == 0:
        other = swap_lanes(value, 1)
        low = jnp.where(bit(1, height), other, value)
        high = jnp.where(bit(1, height), value, other)
        return [low, low, high, high]
    outer, inner = (2, 1) if level == 1 else (4, 2)
    other = swap_lanes(value, outer)
    result = []
    for half in (jnp.where(bit(outer, height), other, value), jnp.where(bit(outer, height), value, other)):
        swapped = swap_lanes(half, inner)
        result.append(jnp.where(bit(inner, height), swapped, half))
        result.append(jnp.where(bit(inner, height), half, swapped))
    if level == 2:
        same = bit(2, height) == bit(1, height)
        result = [jnp.where(same, part, swap_lanes(part, 1)) for part in result]
    return result


def pair_rows(tmp, slot, value):
    count = value.shape[0] // 2
    tmp[slot, pl.ds(0, 2 * count)] = value
    summed = tmp[slot, pl.ds(0, count, stride=2)] + tmp[slot, pl.ds(1, count, stride=2)]
    return 0.125 * summed


def restrict(level, plane, target, tmp, fine_x, planes, count, at_x, at_row, limit=None):
    def one(i):
        parts = [fine_x + 4 * i + m for m in range(4)]
        if limit is not None:
            parts = [min(part, limit) for part in parts]
        value = coarsen(level, [plane(part) for part in parts])
        target[at_x + i, pl.ds(at_row, count)] = pair_rows(tmp, i, value)

    if level == 2:
        for i in range(planes):
            one(i)
    else:
        loop(0, planes, one, 1)


def field_plane(b, fine_row, count):
    return lambda x: b[x, pl.ds(fine_row, 2 * count)]


def residual_plane(level, u, f, cx, cxm, cy, cz, diag, fine_row, count):
    span = pl.ds(0, ROWS[level])

    def left(x):
        here, total = spread(level, x, u, cx, cxm, cy, cz, span)
        return (f[x] + total - diag[x] * here)[fine_row : fine_row + 2 * count]

    return left


def add_coarse(level, u, coarse, tmp, first, last, fine_x, coarse_row, fine_row, count, keep=None):
    def one(i):
        trip = i - first
        value = coarse[i, pl.ds(coarse_row, count)]
        tmp[trip, pl.ds(0, count, stride=2)] = value
        tmp[trip, pl.ds(1, count, stride=2)] = value
        span = pl.ds(fine_row, 2 * count)
        for m, part in enumerate(refine(level, tmp[trip, pl.ds(0, 2 * count)])):
            x = fine_x + 4 * trip + m
            if keep is None or x in keep:
                u[x, span] = u[x, span] + part

    if level == 2:
        for i in range(first, last):
            one(i)
    else:
        loop(first, last, one, 1)


def side(offset, length, width, at):
    if offset == 0:
        return pl.ds(0, length), pl.ds(at, length)
    if offset == 1:
        return pl.ds(length - width, width), pl.ds(at - width, width)
    return pl.ds(0, width), pl.ds(at + length, width)


def kernel(nx, ny, f_in, b_in, out, *refs):
    fields = [refs[10 * level : 10 * level + 10] for level in range(4)]
    tmp, load_sem, send_sem, recv_sem = refs[40:]
    (b0, f0, u0, v0, cx0, cm0, cy0, cz0, d0, g0) = fields[0]
    (b1, f1, u1, v1, cx1, cm1, cy1, cz1, d1, g1) = fields[1]
    (b2, f2, u2, v2, cx2, cm2, cy2, cz2, d2, g2) = fields[2]
    (b3, f3, u3, v3, cx3, cm3, cy3, cz3, d3, g3) = fields[3]
    c0, c1, c2, c3 = [(level[4], level[5], level[6], level[7]) for level in fields]
    mx, my = lax.axis_index("gx"), lax.axis_index("gy")
    far = [(dx, dy) for dx in far_offsets(nx) for dy in (-2, -1, 0, 1, 2) if (dx, dy) != (0, 0)]

    def peer(dx, dy):
        return (lax.rem(mx + dx + nx, nx), lax.rem(my + dy + ny, ny))

    barrier = pltpu.get_barrier_semaphore()
    greet = sorted(set(far) | set((-dx, -dy) for dx, dy in far))
    for dx, dy in greet:
        pl.semaphore_signal(barrier, inc=1, device_id=peer(dx, dy), device_id_type=MESH)

    inside = (pl.ds(5, OWN), pl.ds(8, OWN))
    load_b = pltpu.make_async_copy(b_in, b0.at[inside], load_sem.at[0])
    load_f = pltpu.make_async_copy(f_in, f0.at[inside], load_sem.at[1])
    load_b.start()
    load_f.start()
    pl.semaphore_wait(barrier, len(greet))

    started = []

    def send(source, target, dx, dy):
        number = len(started)
        copy = pltpu.make_async_remote_copy(
            src_ref=source,
            dst_ref=target,
            send_sem=send_sem.at[number],
            recv_sem=recv_sem.at[number],
            device_id=peer(dx, dy),
            device_id_type=MESH,
        )
        copy.start()
        started.append(copy)
        return copy

    fine = []
    for dx, dy in NEAR:
        for source, target, width in ((b_in, b0, 5), (f_in, f0, 4)):
            from_x, to_x = side(dx, OWN, width - (dy != 0), 5)
            from_y, to_y = side(dy, OWN, 8, 8)
            fine.append(send(source.at[from_x, from_y], target.at[to_x, to_y], dx, dy))

    def send_1(field):
        copies = []
        for dx, dy in NEAR:
            from_x, to_x = side(dx, 8, 3, 4)
            from_y, to_y = side(dy, 16, 8, 8)
            from_x = pl.ds(from_x.start + 4, from_x.size)
            from_y = pl.ds(from_y.start + 8, from_y.size)
            copies.append(send(field.at[from_x, from_y], field.at[to_x, to_y], dx, dy))
        return copies

    def block_2(field, dx, dy):
        return field.at[pl.ds(5 + 2 * dx, 2), pl.ds(16 + 8 * dy, 8)]

    def send_2(field):
        return [send(block_2(field, 0, 0), block_2(field, -dx, -dy), dx, dy) for dx, dy in far]

    def finish_2(field, copies):
        for copy in copies:
            copy.wait_recv()
        if nx == 4:
            for p in (1, 2):
                field[p + 8] = field[p]

    load_b.wait()
    restrict(0, field_plane(b0, 8, 16), b1, tmp, 5, 8, 16, 4, 8)
    middle_b = send_1(b1)
    restrict(1, field_plane(b1, 8, 8), b2, tmp, 4, 2, 8, 5, 16)
    coarse_b = send_2(b2)
    load_f.wait()
    for copy in fine:
        copy.wait_recv()

    build(0, b0, f0, *c0, d0, g0, u0)
    sweep(0, 2, 40, u0, v0, f0, *c0, g0)
    sweep(0, 3, 39, v0, u0, f0, *c0, g0)
    restrict(0, residual_plane(0, u0, f0, *c0, d0, 8, 16), f1, tmp, 5, 8, 16, 4, 8)
    middle_f = send_1(f1)
    for copy in middle_b:
        copy.wait_recv()
    for copy in middle_f:
        copy.wait_recv()

    build(1, b1, f1, *c1, d1, g1, u1)
    sweep(1, 1, 15, u1, v1, f1, *c1, g1)
    sweep(1, 1, 15, v1, u1, f1, *c1, g1)
    restrict(1, residual_plane(1, u1, f1, *c1, d1, 8, 8), f2, tmp, 4, 2, 8, 5, 16)
    coarse_f = send_2(f2)
    finish_2(b2, coarse_b)
    restrict(2, field_plane(b2, 0, 20), b3, tmp, 1, 3, 20, 1, 0, 10)
    finish_2(f2, coarse_f)

    build(2, b2, f2, *c2, d2, g2, u2)
    sweep(2, 1, 11, u2, v2, f2, *c2, g2)
    sweep(2, 1, 11, v2, u2, f2, *c2, g2)
    restrict(2, residual_plane(2, u2, f2, *c2, d2, 0, 20), f3, tmp, 1, 3, 20, 1, 0, 10)

    build(3, b3, f3, *c3, d3, g3, u3)
    sweep(3, 1, 4, u3, v3, f3, *c3, g3)
    sweep(3, 1, 4, v3, u3, f3, *c3, g3)
    sweep(3, 1, 4, u3, v3, f3, *c3, g3)
    sweep(3, 1, 4, v3, u3, f3, *c3, g3)

    add_coarse(2, u2, u3, tmp, 1, 3, 1, 4, 8, 12, (4, 5, 6, 7))
    middle = pl.ds(8, 24)
    sweep(2, 4, 8, u2, v2, f2, *c2, g2, middle)
    sweep(2, 4, 8, v2, u2, f2, *c2, g2, middle)

    add_coarse(1, u1, u2, tmp, 4, 8, 0, 12, 0, 16)
    sweep(1, 2, 14, u1, v1, f1, *c1, g1)
    sweep(1, 3, 13, v1, u1, f1, *c1, g1)

    add_coarse(0, u0, u1, tmp, 3, 13, 1, 4, 0, 24)
    sweep(0, 4, 38, u0, v0, f0, *c0, g0)

    whole = pl.ds(0, ROWS[0])

    def last(x):
        here, total = spread(0, x, v0, *c0, whole)
        value = (1.0 - OMEGA) * here + g0[x] * (f0[x] + total)
        out[x - 5] = value[8:40]

    loop(5, 37, last)
    for copy in started:
        copy.wait_send()


def solution(mesh):
    nx, ny = mesh.shape["gx"], mesh.shape["gy"]
    far = len(far_offsets(nx)) * 5 - 1
    copies = 4 * len(NEAR) + 2 * far
    shapes = []
    for planes, height in zip(PLANES, ROWS):
        shapes += [pltpu.VMEM((planes, height, 128), F32)] * 10

    def per_device(source, inverse_density):
        return pl.pallas_call(
            functools.partial(kernel, nx, ny),
            out_shape=jax.ShapeDtypeStruct(source.shape, F32),
            in_specs=[pl.BlockSpec(memory_space=pl.ANY)] * 2,
            out_specs=pl.BlockSpec(memory_space=pltpu.VMEM),
            scratch_shapes=shapes
            + [
                pltpu.VMEM((20, 48, 128), F32),
                pltpu.SemaphoreType.DMA((2,)),
                pltpu.SemaphoreType.DMA((copies,)),
                pltpu.SemaphoreType.DMA((copies,)),
            ],
            compiler_params=pltpu.CompilerParams(collective_id=0, has_side_effects=True),
        )(source, inverse_density)

    placed = (P("gx", "gy", None), P("gx", "gy", None))
    return jax.shard_map(
        per_device, mesh=mesh, in_specs=placed, out_specs=P("gx", "gy", None), check_vma=False
    )
```

time: 70.5 us -> 57.9 us (0.82)
  Pallas kernels: 68.5 us -> 55.9 us
    pallas_call x1, Pallas kernels: 68.5 us -> 55.9 us  [per_device(): pl.pallas_call(functools.partial(kernel, nx, ny), out_shape=jax.ShapeDtyp...]
where the time goes in v2:
time: 57.9 us; the launch traced here: 57.8 us
  Pallas kernels  55.9 us (97%)
  local copies, waits for them, and re-layouts  1.87 us (3%)
    pallas_call x1, Pallas kernels, per_device(): pl.pallas_call(functools.partial(kernel, nx, ny), out_shape=jax.ShapeDtyp...  55.9 us
    unnamed x1, local copies, waits for them, and re-layouts  1.87 us

profile of v2, /device:TPU:0, one launch (start us, length us, event | category | flops | bytes accessed | tf_op | source)
XLA Modules:
  0.0 57.8 jit_solution(14621712526645747937)
XLA Ops:
  0.0 55.9 %shard_map.28 = f32[32,32,128]{2,1,0:T(8,128)} custom-call(f32[32,32,128]{2,1,0:T(8,128)} %f_in.1, f32[32,32,128]{2,1,0:T(8,128)} %b_in.1), custom_call_target="tpu_custom_call" | custom-call | tf_op jit(solution)/shard_map/pallas_call | solution.py:400
  55.9 1.9 %copy.4 = f32[32,32,128]{2,1,0:T(8,128)} copy(f32[32,32,128]{2,1,0:T(8,128)} %shard_map.28) | data formatting | bytes 1048576

commit v3 on v2

--- a/solution.py
+++ b/solution.py
@@ -13,6 +13,7 @@
 
 PLANES = (42, 16, 12, 5)
 ROWS = (48, 32, 40, 24)
+UNROLL = (4, 7, 5, 3)
 OWN = 32
 NEAR = [(dx, dy) for dx in (1, -1, 0) for dy in (0, 1, -1) if (dx, dy) != (0, 0)]
 
@@ -40,14 +41,15 @@
 
 def loop(first, last, body, unroll=2):
     count = last - first
-    whole = count // unroll
+    whole = count // unroll if count > unroll else 0
 
     def step(trip, carry):
         for inner in range(unroll):
             body(first + trip * unroll + inner)
         return carry
 
-    lax.fori_loop(0, whole, step, 0)
+    if whole:
+        lax.fori_loop(0, whole, step, 0)
     for index in range(first + whole * unroll, last):
         body(index)
 
@@ -76,7 +78,7 @@
     return jnp.where(first, lanes(before, 1 - size), lanes(here, 1))
 
 
-def build(level, b, f, cx, cxm, cy, cz, diag, gain, u):
+def build(level, first, last, b, cx, cxm, cy, cz, diag, gain, f=None, u=None):
     height = ROWS[level]
     factor2 = 2.0 * 0.25**level
     step = 2**level
@@ -104,23 +106,31 @@
         cz[x] = c_z
         diag[x] = total
         gain[x] = scaled
-        u[x] = scaled * f[x]
+        if f is not None:
+            u[x] = scaled * f[x]
         return (c_x, after)
 
-    first = pair(b[0], next_x(level, b[0], b[1]))
-    cx[0] = first
-    count = PLANES[level] - 2
-    carry = (first, b[1])
-    if level == 3:
-        for x in range(1, 1 + count):
+    before = pair(b[first - 1], next_x(level, b[first - 1], b[first]))
+    cx[first - 1] = before
+    count = last - first
+    carry = (before, b[first])
+    if count < 6:
+        for x in range(first, last):
             carry = one(x, carry)
         return
 
     def two(trip, carry):
-        carry = one(1 + 2 * trip, carry)
-        return one(2 + 2 * trip, carry)
+        carry = one(first + 2 * trip, carry)
+        return one(first + 1 + 2 * trip, carry)
 
     lax.fori_loop(0, count // 2, two, carry)
+
+
+def first_sweep(level, first, last, u, f, gain):
+    def one(x):
+        u[x] = gain[x] * f[x]
+
+    loop(first, last, one, UNROLL[level])
 
 
 def spread(level, x, u, cx, cxm, cy, cz, span):
@@ -143,11 +153,7 @@
         here, total = spread(level, x, source, cx, cxm, cy, cz, span)
         target[x, span] = (1.0 - OMEGA) * here + gain[x, span] * (f[x, span] + total)
 
-    if level == 3:
-        for x in range(first, last):
-            one(x)
-    else:
-        loop(first, last, one)
+    loop(first, last, one, UNROLL[level])
 
 
 def coarsen(level, values):
@@ -209,7 +215,7 @@
         for i in range(planes):
             one(i)
     else:
-        loop(0, planes, one, 1)
+        loop(0, planes, one, 2)
 
 
 def field_plane(b, fine_row, count):
@@ -242,7 +248,7 @@
         for i in range(first, last):
             one(i)
     else:
-        loop(first, last, one, 1)
+        loop(first, last, one, 2)
 
 
 def side(offset, length, width, at):
@@ -295,12 +301,30 @@
         started.append(copy)
         return copy
 
-    fine = []
-    for dx, dy in NEAR:
-        for source, target, width in ((b_in, b0, 5), (f_in, f0, 4)):
-            from_x, to_x = side(dx, OWN, width - (dy != 0), 5)
+    def send_0(dx, dy, wide, skip=0):
+        copies = []
+        for source, target, width in ((b_in, b0, wide), (f_in, f0, wide - 1)):
+            from_x, to_x = side(dx, OWN, width, 5)
+            if skip:
+                count = 1
+                if dx == 1:
+                    from_x, to_x = pl.ds(from_x.start, count), pl.ds(to_x.start, count)
+                else:
+                    from_x = pl.ds(width - 1, count)
+                    to_x = pl.ds(5 + OWN + width - 1, count)
             from_y, to_y = side(dy, OWN, 8, 8)
-            fine.append(send(source.at[from_x, from_y], target.at[to_x, to_y], dx, dy))
+            copies.append(send(source.at[from_x, from_y], target.at[to_x, to_y], dx, dy))
+        return copies
+
+    def arrive(copies):
+        for copy in copies:
+            copy.wait_recv()
+
+    along_y = send_0(0, 1, 5) + send_0(0, -1, 5)
+    along_x = send_0(1, 0, 4) + send_0(-1, 0, 4)
+    for dx in (1, -1):
+        for dy in (1, -1):
+            along_x += send_0(dx, dy, 4)
 
     def send_1(field):
         copies = []
@@ -315,8 +339,12 @@
     def block_2(field, dx, dy):
         return field.at[pl.ds(5 + 2 * dx, 2), pl.ds(16 + 8 * dy, 8)]
 
-    def send_2(field):
-        return [send(block_2(field, 0, 0), block_2(field, -dx, -dy), dx, dy) for dx, dy in far]
+    def send_2(field, corners):
+        return [
+            send(block_2(field, 0, 0), block_2(field, -dx, -dy), dx, dy)
+            for dx, dy in far
+            if corners or abs(dx) + abs(dy) < 4
+        ]
 
     def finish_2(field, copies):
         for copy in copies:
@@ -327,38 +355,52 @@
 
     load_b.wait()
     restrict(0, field_plane(b0, 8, 16), b1, tmp, 5, 8, 16, 4, 8)
+    restrict(1, field_plane(b1, 8, 8), b2, tmp, 4, 2, 8, 5, 16)
+    load_f.wait()
+    arrive(along_y)
+    build(0, 6, 36, b0, *c0, d0, g0, f0, u0)
+    sweep(0, 7, 35, u0, v0, f0, *c0, g0)
+    arrive(along_x)
     middle_b = send_1(b1)
-    restrict(1, field_plane(b1, 8, 8), b2, tmp, 4, 2, 8, 5, 16)
-    coarse_b = send_2(b2)
-    load_f.wait()
-    for copy in fine:
-        copy.wait_recv()
-
-    build(0, b0, f0, *c0, d0, g0, u0)
-    sweep(0, 2, 40, u0, v0, f0, *c0, g0)
-    sweep(0, 3, 39, v0, u0, f0, *c0, g0)
+    outer = []
+    for dx in (1, -1):
+        outer += send_0(dx, 0, 5, 1)
+    build(0, 2, 6, b0, *c0, d0, g0, f0, u0)
+    build(0, 36, 40, b0, *c0, d0, g0, f0, u0)
+    sweep(0, 3, 7, u0, v0, f0, *c0, g0)
+    sweep(0, 35, 39, u0, v0, f0, *c0, g0)
+    sweep(0, 4, 38, v0, u0, f0, *c0, g0)
     restrict(0, residual_plane(0, u0, f0, *c0, d0, 8, 16), f1, tmp, 5, 8, 16, 4, 8)
     middle_f = send_1(f1)
-    for copy in middle_b:
-        copy.wait_recv()
-    for copy in middle_f:
-        copy.wait_recv()
-
-    build(1, b1, f1, *c1, d1, g1, u1)
+    arrive(middle_b)
+    build(1, 1, 15, b1, *c1, d1, g1)
+    arrive(outer)
+    build(0, 1, 2, b0, *c0, d0, g0, f0, u0)
+    build(0, 40, 41, b0, *c0, d0, g0, f0, u0)
+    for x in (2, 39):
+        sweep(0, x, x + 1, u0, v0, f0, *c0, g0)
+    for x in (3, 38):
+        sweep(0, x, x + 1, v0, u0, f0, *c0, g0)
+    arrive(middle_f)
+    coarse_b = send_2(b2, True)
+
+    first_sweep(1, 1, 15, u1, f1, g1)
     sweep(1, 1, 15, u1, v1, f1, *c1, g1)
     sweep(1, 1, 15, v1, u1, f1, *c1, g1)
     restrict(1, residual_plane(1, u1, f1, *c1, d1, 8, 8), f2, tmp, 4, 2, 8, 5, 16)
-    coarse_f = send_2(f2)
+    coarse_f = send_2(f2, False)
     finish_2(b2, coarse_b)
     restrict(2, field_plane(b2, 0, 20), b3, tmp, 1, 3, 20, 1, 0, 10)
+    build(2, 1, 11, b2, *c2, d2, g2)
+    build(3, 1, 4, b3, *c3, d3, g3)
     finish_2(f2, coarse_f)
 
-    build(2, b2, f2, *c2, d2, g2, u2)
+    first_sweep(2, 1, 11, u2, f2, g2)
     sweep(2, 1, 11, u2, v2, f2, *c2, g2)
     sweep(2, 1, 11, v2, u2, f2, *c2, g2)
     restrict(2, residual_plane(2, u2, f2, *c2, d2, 0, 20), f3, tmp, 1, 3, 20, 1, 0, 10)
 
-    build(3, b3, f3, *c3, d3, g3, u3)
+    first_sweep(3, 1, 4, u3, f3, g3)
     sweep(3, 1, 4, u3, v3, f3, *c3, g3)
     sweep(3, 1, 4, v3, u3, f3, *c3, g3)
     sweep(3, 1, 4, u3, v3, f3, *c3, g3)
@@ -383,7 +425,7 @@
         value = (1.0 - OMEGA) * here + g0[x] * (f0[x] + total)
         out[x - 5] = value[8:40]
 
-    loop(5, 37, last)
+    loop(5, 37, last, 4)
     for copy in started:
         copy.wait_send()
 
@@ -391,7 +433,7 @@
 def solution(mesh):
     nx, ny = mesh.shape["gx"], mesh.shape["gy"]
     far = len(far_offsets(nx)) * 5 - 1
-    copies = 4 * len(NEAR) + 2 * far
+    copies = 20 + 2 * len(NEAR) + 2 * far
     shapes = []
     for planes, height in zip(PLANES, ROWS):
         shapes += [pltpu.VMEM((planes, height, 128), F32)] * 10

time: 57.9 us -> 46.9 us (0.81)
  Pallas kernels: 55.9 us -> 44.8 us
    pallas_call x1, Pallas kernels: 55.9 us -> 44.8 us  [per_device(): pl.pallas_call(functools.partial(kernel, nx, ny), out_shape=jax.ShapeDtyp...]
where the time goes in v3:
time: 46.9 us; the launch traced here: 46.7 us
  Pallas kernels  44.8 us (96%)
  local copies, waits for them, and re-layouts  1.87 us (4%)
    pallas_call x1, Pallas kernels, per_device(): pl.pallas_call(functools.partial(kernel, nx, ny), out_shape=jax.ShapeDtyp...  44.8 us
    unnamed x1, local copies, waits for them, and re-layouts  1.87 us

profile of v3, /device:TPU:0, one launch (start us, length us, event | category | flops | bytes accessed | tf_op | source)
XLA Modules:
  0.0 46.7 jit_solution(4974751886604179899)
XLA Ops:
  0.0 44.8 %shard_map.28 = f32[32,32,128]{2,1,0:T(8,128)} custom-call(f32[32,32,128]{2,1,0:T(8,128)} %f_in.1, f32[32,32,128]{2,1,0:T(8,128)} %b_in.1), custom_call_target="tpu_custom_call" | custom-call | tf_op jit(solution)/shard_map/pallas_call | solution.py:442
  44.9 1.9 %copy.4 = f32[32,32,128]{2,1,0:T(8,128)} copy(f32[32,32,128]{2,1,0:T(8,128)} %shard_map.28) | data formatting | bytes 1048576

commit v4 on v3

--- a/solution.py
+++ b/solution.py
@@ -274,8 +274,7 @@
         return (lax.rem(mx + dx + nx, nx), lax.rem(my + dy + ny, ny))
 
     barrier = pltpu.get_barrier_semaphore()
-    greet = sorted(set(far) | set((-dx, -dy) for dx, dy in far))
-    for dx, dy in greet:
+    for dx, dy in NEAR:
         pl.semaphore_signal(barrier, inc=1, device_id=peer(dx, dy), device_id_type=MESH)
 
     inside = (pl.ds(5, OWN), pl.ds(8, OWN))
@@ -283,7 +282,7 @@
     load_f = pltpu.make_async_copy(f_in, f0.at[inside], load_sem.at[1])
     load_b.start()
     load_f.start()
-    pl.semaphore_wait(barrier, len(greet))
+    pl.semaphore_wait(barrier, len(NEAR))
 
     started = []
 
@@ -312,7 +311,7 @@
                 else:
                     from_x = pl.ds(width - 1, count)
                     to_x = pl.ds(5 + OWN + width - 1, count)
-            from_y, to_y = side(dy, OWN, 8, 8)
+            from_y, to_y = side(dy, OWN, width, 8)
             copies.append(send(source.at[from_x, from_y], target.at[to_x, to_y], dx, dy))
         return copies
 
@@ -365,6 +364,7 @@
     outer = []
     for dx in (1, -1):
         outer += send_0(dx, 0, 5, 1)
+    coarse_b = send_2(b2, True)
     build(0, 2, 6, b0, *c0, d0, g0, f0, u0)
     build(0, 36, 40, b0, *c0, d0, g0, f0, u0)
     sweep(0, 3, 7, u0, v0, f0, *c0, g0)
@@ -382,7 +382,6 @@
     for x in (3, 38):
         sweep(0, x, x + 1, v0, u0, f0, *c0, g0)
     arrive(middle_f)
-    coarse_b = send_2(b2, True)
 
     first_sweep(1, 1, 15, u1, f1, g1)
     sweep(1, 1, 15, u1, v1, f1, *c1, g1)

time: 46.9 us -> 44.9 us (0.957)
  Pallas kernels: 44.8 us -> 42.9 us
    pallas_call x1, Pallas kernels: 44.8 us -> 42.9 us  [per_device(): pl.pallas_call(functools.partial(kernel, nx, ny), out_shape=jax.ShapeDtyp...]
where the time goes in v4:
time: 44.9 us; the launch traced here: 44.7 us
  Pallas kernels  42.9 us (96%)
  local copies, waits for them, and re-layouts  1.87 us (4%)
    pallas_call x1, Pallas kernels, per_device(): pl.pallas_call(functools.partial(kernel, nx, ny), out_shape=jax.ShapeDtyp...  42.9 us
    unnamed x1, local copies, waits for them, and re-layouts  1.87 us

profile of v4, /device:TPU:0, one launch (start us, length us, event | category | flops | bytes accessed | tf_op | source)
XLA Modules:
  0.0 44.7 jit_solution(7259928731550819055)
XLA Ops:
  0.0 42.9 %shard_map.28 = f32[32,32,128]{2,1,0:T(8,128)} custom-call(f32[32,32,128]{2,1,0:T(8,128)} %f_in.1, f32[32,32,128]{2,1,0:T(8,128)} %b_in.1), custom_call_target="tpu_custom_call" | custom-call | tf_op jit(solution)/shard_map/pallas_call | solution.py:441
  42.9 1.9 %copy.4 = f32[32,32,128]{2,1,0:T(8,128)} copy(f32[32,32,128]{2,1,0:T(8,128)} %shard_map.28) | data formatting | bytes 1048576
